TPU v7x, 32 devices: a whole 2x2x4 slice. The times are simulated.
32 devices in a mesh: rep: 2 (over x), idx: 16 (over z, y, core).
Axes of the slice: x: 2, y: 2, z: 4, core: 2. Of those that a mesh axis runs over, the one named last changes fastest.
Arguments:
- images: bfloat16 [16448, 1408], P(('rep', 'idx')), parts along dimension 0, may hold values from -6 to 6
- norm_gain: float32 [1408], replicated, may hold values from 0.25 to 1.75
- qkv_values: bfloat16 [1408, 4224], P(None, 'idx'), may hold values from -0.5 to 0.5
- qkv_exponents: int32 [11, 4224], replicated, may hold values from -2 to 2
- proj_values: bfloat16 [1408, 1408], P(None, 'idx'), may hold values from -0.078125 to 0.078125
- proj_exponents: int32 [11, 1408], replicated, may hold values from -2 to 2
- captions: bfloat16 [32768, 1408], P(('rep', 'idx')), parts along dimension 0, may hold values from -0.15625 to 0.15625
- owners: int32 [16448, 1], P(('rep', 'idx')), parts along dimension 0, may hold values from 0 to 15; in each aligned block of 514 rows (0 to 513, 514 to 1027, ...) at most 34 rows name the same one
- candidates: int32 [16448, 4], P(('rep', 'idx')), parts along dimension 0, may hold values from 0 to 7, all different within a row
Outputs:
- embedding: bfloat16 [16448, 1408], P(('rep', 'idx')), parts along dimension 0
- scores: bfloat16 [16448, 4, 128], P(('rep', 'idx')), parts along dimension 0
There are 2 independent parts, one for each index of `rep`. A program takes and returns all parts, laid end to end along the dimension named above; an argument that names none is the same for every part. Nothing has to cross between parts.
Inputs may be any that keep to these rules, and one draw needn't show every extreme that they name: `owners`: among the tokens of one device no owner is named more than 34 times, a bound that some block reaches. `candidates`: each token names 4 different caption blocks.
All inputs are finite; a program needn't handle non-finite values.
Results may differ from a plain program's by a relative error of at most 0.004.
The roundings to bfloat16 on the way count: a program that leaves them out, or rounds other values in their place, can miss the bound.
Values may be sent and summed in bfloat16 or wider, within the bound.
A program may use at most 192 MiB of HBM per device.

v0:
```python
import math
import jax
import jax.numpy as jnp
from jax import lax
from jax.experimental import pallas as pl
from jax.experimental.pallas import tpu as pltpu
from jax.sharding import PartitionSpec as P

HEADS = 16
PATCHES = 257
CBLK = 8
CAPT = 128
F32 = jnp.float32
BF16 = jnp.bfloat16
VMEM = pltpu.VMEM
VLIMIT = 60 * 1024 * 1024


def dequant_rows(stored, exponents):
    row_count, col_count = stored.shape
    block_count = exponents.shape[0]
    turned = stored.T.astype(F32).reshape(col_count, block_count, row_count // block_count)
    scaled = turned * jnp.exp2(exponents.astype(F32)).T[:, :, None]
    return scaled.reshape(col_count, row_count).astype(BF16)


def layer_norm(token_rows, norm_gain):
    values = token_rows.astype(F32)
    centered = values - jnp.mean(values, axis=-1, keepdims=True)
    inv_scale = lax.rsqrt(jnp.mean(centered * centered, axis=-1, keepdims=True) + 1e-06)
    return (centered * inv_scale * norm_gain).astype(BF16)


def dot_nt(left, right):
    return lax.dot_general(left, right, (((1,), (1,)), ((), ())), preferred_element_type=F32)


MESH = pl.DeviceIdType.MESH
SHARE = 11


def gather_kernel(q_own, p_own, q_out, p_out, q_hold, p_hold, rz, ry, rx, rc, sz, sy, sx, sc, held):
    peers = q_out.shape[0]
    nz = peers // 4
    me = lax.axis_index("idx")
    x = lax.axis_index("rep")
    z, y, c = me // 4, (me // 2) % 2, me % 2
    own, out = (q_own, p_own), (q_out, p_out)

    def at(zz, yy, cc):
        return (zz * 2 + yy) * 2 + cc

    to_y, to_c, to_x = (x, at(z, 1 - y, c)), (x, at(z, y, 1 - c)), (1 - x, me)
    to_up, to_down = (x, me + 4), (x, me - 4)

    barrier = pltpu.get_barrier_semaphore()

    def greet(target):
        pl.semaphore_signal(barrier, inc=1, device_id=target, device_id_type=MESH)

    for target in (to_y, to_c, to_x):
        greet(target)

    @pl.when(z + 1 < nz)
    def _():
        greet(to_up)

    @pl.when(z > 0)
    def _():
        greet(to_down)

    greeted = 3 + jnp.where(z + 1 < nz, 1, 0) + jnp.where(z > 0, 1, 0)
    pl.semaphore_wait(barrier, greeted)

    def rows(a, k):
        unit = own[a].shape[0] // SHARE
        if k == 0:
            return pl.ds(0, 3 * unit)
        if k == 3:
            return pl.ds(0, SHARE * unit)
        side = x if k == 1 else 1 - x
        return pl.ds(pl.multiple_of((3 + 4 * side) * unit, 8), 4 * unit)

    def copy(a, shard, k, mine, send, recv, target):
        span = rows(a, k)
        return pltpu.make_async_remote_copy(
            src_ref=own[a].at[span] if mine else out[a].at[shard, span],
            dst_ref=out[a].at[shard, span],
            send_sem=send,
            recv_sem=recv,
            device_id=target,
            device_id_type=MESH,
        )

    def pos(zz, yy):
        return zz * 2 + yy

    def up(a, zz, k, mine=False):
        return copy(a, at(zz, y, c), k, mine, sz.at[0, a, zz, k], rz.at[a, zz, k], to_up)

    def down(a, zz, k, mine=False):
        return copy(a, at(zz, y, c), k, mine, sz.at[1, a, zz, k], rz.at[a, zz, k], to_down)

    def across(a, zz, k, yy, mine=False):
        return copy(a, at(zz, yy, c), k, mine, sy.at[a, zz, k], ry.at[a, zz, k], to_y)

    def plane(a, zz, yy, k):
        return copy(a, at(zz, yy, c), k, False, sx.at[a, pos(zz, yy)], rx.at[a, pos(zz, yy)], to_x)

    def core(a, zz, yy, cc, k, mine=False):
        slot = 0 if k == 3 else k
        return copy(
            a, at(zz, yy, cc), k, mine, sc.at[a, pos(zz, yy), slot], rc.at[a, pos(zz, yy), slot], to_c
        )

    def each(distance, body):
        if distance == 0:
            body(z, 0)
            return

        @pl.when(z - distance >= 0)
        def _():
            body(z - distance, -1)

        @pl.when(z + distance < nz)
        def _():
            body(z + distance, 1)

    holds = []
    for a in range(2):
        for k in (1, 0):

            @pl.when(z + 1 < nz)
            def _():
                up(a, z, k, True).start()

            @pl.when(z > 0)
            def _():
                down(a, z, k, True).start()

            across(a, z, k, y, True).start()
        core(a, z, y, c, 3, True).start()
        hold = (q_hold, p_hold)[a]
        load = pltpu.make_async_copy(own[a], hold, held.at[a, 0])
        load.start()
        holds.append((load, pltpu.make_async_copy(hold, out[a].at[me], held.at[a, 1])))
    for load, store in holds:
        load.wait()
        store.start()

    for a in range(2):
        for step in range(1, nz + 2):
            if step < nz:

                def from_chain(zz, side):
                    for k in (1, 0):
                        up(a, zz, k).wait_recv()
                        if side < 0:

                            @pl.when(z + 1 < nz)
                            def _():
                                up(a, zz, k).start()
                        else:

                            @pl.when(z > 0)
                            def _():
                                down(a, zz, k).start()

                        across(a, zz, k, y).start()
                        if k == 1:
                            plane(a, zz, y, 1).start()
                        core(a, zz, y, c, k).start()

                each(step, from_chain)
            if step <= nz:

                def from_across(zz, side):
                    for k in (1, 0):
                        across(a, zz, k, 1 - y).wait_recv()
                        if k == 1:
                            plane(a, zz, 1 - y, 1).start()
                        core(a, zz, 1 - y, c, k).start()

                each(step - 1, from_across)
            if step >= 2:

                def from_plane(zz, side):
                    if side != 0:
                        plane(a, zz, y, 2).wait_recv()
                        core(a, zz, y, c, 2).start()
                    plane(a, zz, 1 - y, 2).wait_recv()
                    core(a, zz, 1 - y, c, 2).start()

                each(step - 2, from_plane)

    for a in range(2):
        for distance in range(nz):

            def finish(zz, side):
                first = side == 0
                for k in (1, 0):
                    if side <= 0:

                        @pl.when(z + 1 < nz)
                        def _():
                            up(a, zz, k, first).wait_send()

                    if side >= 0:

                        @pl.when(z > 0)
                        def _():
                            down(a, zz, k, first).wait_send()

                    across(a, zz, k, y, first).wait_send()
                for yy, mine in ((y, first), (1 - y, False)):
                    if mine:
                        core(a, zz, yy, c, 3, True).wait_send()
                        core(a, zz, yy, 1 - c, 3).wait_recv()
                        continue
                    plane(a, zz, yy, 1).wait_send()
                    for k in (1, 0, 2):
                        core(a, zz, yy, c, k).wait_send()
                        core(a, zz, yy, 1 - c, k).wait_recv()

            each(distance, finish)
    for load, store in holds:
        store.wait()


def gather_call(q_own, p_own, peers):
    anywhere = pl.BlockSpec(memory_space=pl.ANY)
    nz = peers // 4
    dma = pltpu.SemaphoreType.DMA
    return pl.pallas_call(
        gather_kernel,
        in_specs=[anywhere] * 2,
        out_specs=(anywhere, anywhere),
        out_shape=tuple(jax.ShapeDtypeStruct((peers,) + own.shape, own.dtype) for own in (q_own, p_own)),
        scratch_shapes=[
            pltpu.VMEM(q_own.shape, q_own.dtype),
            pltpu.VMEM(p_own.shape, p_own.dtype),
            dma((2, nz, 2)),
            dma((2, nz, 2)),
            dma((2, 2 * nz)),
            dma((2, 2 * nz, 3)),
            dma((2, 2, nz, 2)),
            dma((2, nz, 2)),
            dma((2, 2 * nz)),
            dma((2, 2 * nz, 3)),
            dma((2, 2)),
        ],
        compiler_params=pltpu.CompilerParams(
            collective_id=0, has_side_effects=True, vmem_limit_bytes=4 * 1024 * 1024
        ),
        name="gather_weights",
    )(q_own, p_own)


def gather_rows(q_own, p_own, peers, reps):
    fits = all(own.shape[0] % (8 * SHARE) == 0 for own in (q_own, p_own))
    if fits and peers % 8 == 0 and reps == 2:
        w_qkv, w_proj = gather_call(q_own, p_own, peers)
        return tuple(w.reshape(-1, w.shape[2]) for w in (w_qkv, w_proj))
    return tuple(lax.all_gather(own, "idx", axis=0, tiled=True) for own in (q_own, p_own))


def qkv_kernel(images_ref, gain_ref, w_ref, out_ref, normed):
    group, unit, head_dim = out_ref.shape[0], out_ref.shape[1], out_ref.shape[2]

    @pl.when(pl.program_id(0) == 0)
    def _():
        normed[...] = layer_norm(images_ref[...], gain_ref[...])

    patches = out_ref.shape[3]
    every = dot_nt(w_ref[...], normed[...])
    for g in range(group):
        rows = every[:, g * patches:(g + 1) * patches]
        out_ref[g] = rows.reshape(unit, head_dim, patches).astype(BF16)


def qkv_call(images, gain, w_rows):
    tokens, width = images.shape
    patches = PATCHES
    group = tokens // patches
    head_dim = width // HEADS
    units = w_rows.shape[0] // head_dim
    step = 4
    return pl.pallas_call(
        qkv_kernel,
        grid=(units // step,),
        in_specs=[
            pl.BlockSpec((tokens, width), lambda i: (0, 0)),
            pl.BlockSpec((1, width), lambda i: (0, 0)),
            pl.BlockSpec((step * head_dim, width), lambda i: (i, 0)),
        ],
        out_specs=pl.BlockSpec((group, step, head_dim, patches), lambda i: (0, i, 0, 0)),
        out_shape=jax.ShapeDtypeStruct((group, units, head_dim, patches), BF16),
        scratch_shapes=[pltpu.VMEM((tokens, width), BF16)],
        compiler_params=pltpu.CompilerParams(vmem_limit_bytes=VLIMIT),
        name="qkv",
    )(images, gain, w_rows)


def attend_kernel(qkv_ref, proj_ref, images_ref, slot_ref, emb_ref, send_ref, mixed):
    group, units, head_dim, patches = qkv_ref.shape
    width = HEADS * head_dim
    scale = head_dim ** (-0.5)
    for g in range(group):

        @pl.loop(0, HEADS, unroll=4)
        def _(h):
            queries, keys, vals = qkv_ref[g, h], qkv_ref[g, HEADS + h], qkv_ref[g, 2 * HEADS + h]
            logits = lax.dot_general(
                keys, queries, (((0,), (0,)), ((), ())), preferred_element_type=F32
            )
            logits = logits * scale
            weights = jnp.exp(logits - jnp.max(logits, axis=0, keepdims=True))
            probs = weights * (1.0 / jnp.sum(weights, axis=0, keepdims=True))
            out = jnp.dot(vals, probs.astype(BF16), preferred_element_type=F32)
            mixed[pl.ds(pl.multiple_of(h * head_dim, 8), head_dim), :] = out

        left = mixed[...].T.astype(BF16)
        hidden = images_ref[g * patches:(g + 1) * patches, :].astype(F32) + dot_nt(left, proj_ref[...])
        inv_scale = lax.rsqrt(jnp.mean(hidden * hidden, axis=-1, keepdims=True) + 1e-06)
        emb_ref[g * patches:(g + 1) * patches, :] = (hidden * inv_scale).astype(BF16)
    slots = math.prod(send_ref.shape[:-1])
    tokens = group * patches
    pick = lax.broadcasted_iota(jnp.int32, (slots, tokens), 0) == slot_ref[...]
    onehot = jnp.where(pick, 1.0, 0.0).astype(BF16)
    sent = jnp.dot(onehot, emb_ref[...], preferred_element_type=F32).astype(BF16)
    if len(send_ref.shape) == 2:
        send_ref[...] = sent
        return
    peers, capacity = send_ref.shape[0], send_ref.shape[1]
    for p in range(peers):
        send_ref[p] = sent[p * capacity:(p + 1) * capacity]


def attend_call(qkv, w_proj, images, slot_row, slot_shape):
    tokens, width = images.shape
    patches = qkv.shape[3]
    group = tokens // patches
    full = pl.BlockSpec(memory_space=VMEM)
    return pl.pallas_call(
        attend_kernel,
        in_specs=[full] * 4,
        out_specs=(full, full),
        out_shape=(
            jax.ShapeDtypeStruct((group * patches, width), BF16),
            jax.ShapeDtypeStruct(slot_shape + (width,), BF16),
        ),
        scratch_shapes=[pltpu.VMEM((width, patches), F32)],
        compiler_params=pltpu.CompilerParams(vmem_limit_bytes=VLIMIT),
        name="attend",
    )(qkv, w_proj, images, slot_row)


def score_kernel(rows_ref, picks_ref, captions_ref, out_ref):
    every = dot_nt(rows_ref[...], captions_ref[...]).astype(BF16)
    for k in range(picks_ref.shape[1]):
        pick = picks_ref[:, k:k + 1].astype(F32)
        chosen = jnp.zeros((every.shape[0], CAPT), F32)
        for b in range(CBLK):
            block = every[:, b * CAPT:(b + 1) * CAPT].astype(F32)
            chosen = jnp.where(pick == float(b), block, chosen)
        out_ref[:, k * CAPT:(k + 1) * CAPT] = chosen.astype(BF16)


def score_call(rows, picks, captions):
    full = pl.BlockSpec(memory_space=VMEM)
    return pl.pallas_call(
        score_kernel,
        in_specs=[full] * 3,
        out_specs=full,
        out_shape=jax.ShapeDtypeStruct((rows.shape[0], picks.shape[1] * CAPT), BF16),
        compiler_params=pltpu.CompilerParams(vmem_limit_bytes=VLIMIT),
        name="score",
    )(rows, picks, captions)


def stride_of(capacity):
    return -(-capacity // 8) * 8


def exchange_kernel(
    rows_ref, picks_ref, captions_ref, got_ref,
    rows_in, picks_in, flat, every, chosen, rs, rr, ps, pr, bs, br, own_sem,
):
    peers, capacity = rows_ref.shape[0], rows_ref.shape[1]
    stride = flat.shape[0] // peers
    pick_count = chosen.shape[2] // CAPT
    me = lax.axis_index("idx")
    rep = lax.axis_index("rep")

    def other(step):
        return (me + step) % peers

    barrier = pltpu.get_barrier_semaphore()
    for step in range(1, peers):
        pl.semaphore_signal(barrier, inc=1, device_id=(rep, other(step)), device_id_type=MESH)
    pl.semaphore_wait(barrier, peers - 1)

    def send(src, dst, send_sems, recv_sems, step):
        return pltpu.make_async_remote_copy(
            src_ref=src.at[other(step)],
            dst_ref=dst.at[me],
            send_sem=send_sems.at[step],
            recv_sem=recv_sems.at[step],
            device_id=(rep, other(step)),
            device_id_type=MESH,
        )

    order = sorted(range(1, peers), key=lambda step: -min(step, peers - step))
    for step in order:
        send(rows_ref, rows_in, rs, rr, step).start()
    for step in order:
        send(picks_ref, picks_in, ps, pr, step).start()
    own_rows = pltpu.make_async_copy(rows_ref.at[me], rows_in.at[me], own_sem.at[0])
    own_picks = pltpu.make_async_copy(picks_ref.at[me], picks_in.at[me], own_sem.at[1])
    own_rows.start()
    own_picks.start()
    own_rows.wait()
    own_picks.wait()
    for step in order:
        send(rows_ref, rows_in, rs, rr, step).wait()
        send(picks_ref, picks_in, ps, pr, step).wait()
    for p in range(peers):
        flat[p * stride:p * stride + capacity, :] = rows_in[p]
    every[...] = dot_nt(flat[...], captions_ref[...])
    for p in range(peers):
        columns = picks_in[p].astype(F32).T
        span = slice(p * stride, p * stride + capacity)
        for k in range(pick_count):
            pick = columns[:capacity, k:k + 1]
            best = jnp.zeros((capacity, CAPT), F32)
            for b in range(CBLK):
                best = jnp.where(pick == float(b), every[span, b * CAPT:(b + 1) * CAPT], best)
            chosen[p, :, k * CAPT:(k + 1) * CAPT] = best.astype(BF16)
    for step in order:
        send(chosen, got_ref, bs, br, step).start()
    own_back = pltpu.make_async_copy(chosen.at[me], got_ref.at[me], own_sem.at[2])
    own_back.start()
    own_back.wait()
    for step in order:
        send(chosen, got_ref, bs, br, step).wait()


def exchange_call(rows, picks, captions, pick_count):
    peers, capacity, width = rows.shape
    full = pl.BlockSpec(memory_space=VMEM)
    flat = peers * stride_of(capacity)
    dma = pltpu.SemaphoreType.DMA
    return pl.pallas_call(
        exchange_kernel,
        in_specs=[full] * 3,
        out_specs=pl.BlockSpec(memory_space=pl.ANY),
        out_shape=jax.ShapeDtypeStruct((peers, capacity, pick_count * CAPT), BF16),
        scratch_shapes=[
            pltpu.VMEM(rows.shape, BF16),
            pltpu.VMEM(picks.shape, BF16),
            pltpu.VMEM((flat, width), BF16),
            pltpu.VMEM((flat, captions.shape[0]), F32),
            pltpu.VMEM((peers, capacity, pick_count * CAPT), BF16),
        ]
        + [dma((peers,))] * 6
        + [dma((3,))],
        compiler_params=pltpu.CompilerParams(
            collective_id=1, has_side_effects=True, vmem_limit_bytes=VLIMIT
        ),
        name="exchange",
    )(rows, picks, captions)


def return_kernel(slot_ref, rows_ref, out_ref, *packed):
    if packed:
        (flat,) = packed
        flat[...] = jnp.zeros_like(flat)
        stride = flat.shape[0] // rows_ref.shape[0]
        for p in range(rows_ref.shape[0]):
            flat[p * stride:p * stride + rows_ref.shape[1], :] = rows_ref[p]
        rows = flat[...]
    else:
        rows = rows_ref[...]
    tokens, slots = out_ref.shape[0], rows.shape[0]
    pick = lax.broadcasted_iota(jnp.int32, (tokens, slots), 1) == slot_ref[...]
    onehot = jnp.where(pick, 1.0, 0.0).astype(BF16)
    got = jnp.dot(onehot, rows, preferred_element_type=F32).astype(BF16)
    for k in range(out_ref.shape[1]):
        out_ref[:, k, :] = got[:, k * CAPT:(k + 1) * CAPT]


def return_call(slot_col, rows, pick_count):
    full = pl.BlockSpec(memory_space=VMEM)
    return pl.pallas_call(
        return_kernel,
        in_specs=[full] * 2,
        out_specs=full,
        out_shape=jax.ShapeDtypeStruct((slot_col.shape[0], pick_count, CAPT), BF16),
        scratch_shapes=[pltpu.VMEM((rows.shape[0] * stride_of(rows.shape[1]), rows.shape[2]), BF16)]
        if rows.ndim == 3
        else [],
        compiler_params=pltpu.CompilerParams(vmem_limit_bytes=VLIMIT),
        name="give_back",
    )(slot_col, rows)


def local(
    images,
    norm_gain,
    qkv_values,
    qkv_exponents,
    proj_values,
    proj_exponents,
    captions,
    owners,
    candidates,
):
    token_count, width = images.shape
    peer_count = lax.axis_size("idx")
    me = lax.axis_index("idx")
    capacity = (token_count + peer_count - 1) // peer_count + 1

    def own_exponents(exponents, cols):
        return lax.dynamic_slice_in_dim(exponents, me * cols, cols, axis=1)

    qkv_cols, proj_cols = qkv_values.shape[1], proj_values.shape[1]
    qkv_own = dequant_rows(qkv_values, own_exponents(qkv_exponents, qkv_cols))
    proj_own = dequant_rows(proj_values, own_exponents(proj_exponents, proj_cols))
    w_qkv, w_proj = gather_rows(qkv_own, proj_own, peer_count, lax.axis_size("rep"))

    owner_ids = owners[:, 0]
    onehot = (owner_ids[:, None] == jnp.arange(peer_count, dtype=jnp.int32)[None, :]).astype(
        jnp.int32
    )
    slot_rank = jnp.sum((jnp.cumsum(onehot, axis=0) - onehot) * onehot, axis=1)
    slot_index = owner_ids * capacity + slot_rank
    slots = peer_count * capacity
    pick_count = candidates.shape[1]
    dispatch = (jnp.arange(slots, dtype=jnp.int32)[:, None] == slot_index[None, :]).astype(BF16)
    send_picks = jnp.dot(dispatch, candidates.astype(BF16), preferred_element_type=F32).astype(BF16)
    qkv = qkv_call(images, norm_gain[None, :], w_qkv)
    if capacity >= 16:
        turned = send_picks.reshape(peer_count, capacity, pick_count).transpose(0, 2, 1)
        turned = jnp.pad(turned, ((0, 0), (0, 16 - pick_count), (0, 128 - capacity)))
        embedding, send_rows = attend_call(
            qkv, w_proj, images, slot_index[None, :], (peer_count, capacity)
        )
        returned = exchange_call(send_rows, turned, captions, pick_count)
        place = owner_ids * stride_of(capacity) + slot_rank
    else:
        embedding, send_rows = attend_call(qkv, w_proj, images, slot_index[None, :], (slots,))

        def swap(blocks):
            shaped = blocks.reshape(peer_count, capacity, blocks.shape[1])
            moved = lax.all_to_all(shaped, "idx", split_axis=0, concat_axis=0, tiled=True)
            return moved.reshape(blocks.shape)

        returned = swap(score_call(swap(send_rows), swap(send_picks), captions))
        place = slot_index
    scores = return_call(place[:, None], returned, pick_count)
    return (embedding, scores)


def solution(mesh):
    placed = (
        P(("rep", "idx"), None),
        P(),
        P(None, "idx"),
        P(),
        P(None, "idx"),
        P(),
        P(("rep", "idx"), None),
        P(("rep", "idx"), None),
        P(("rep", "idx"), None),
    )
    return jax.shard_map(
        local,
        mesh=mesh,
        in_specs=placed,
        out_specs=(P(("rep", "idx"), None), P(("rep", "idx"), None, None)),
        check_vma=False,
    )
```

profile of v0, /device:TPU:0, one launch (start us, length us, event | category | flops | bytes accessed | tf_op | source)
XLA Modules:
  0.0 199.3 jit_solution(1589210549780584424)
XLA Ops:
  0.6 0.9 exponential_bitcast_fusion
  1.6 0.1 copy.23
  1.7 0.6 mul.60
  2.3 0.8 fusion.q_own
  3.1 0.8 exponential_bitcast_fusion.1
  3.9 0.1 copy.24
  4.0 0.3 mul.64
  4.3 0.2 fusion.4.p_own
  4.5 71.5 %gather_weights.1 = (bf16[16,264,1408]{2,1,0:T(8,128)(2,1)S(1)}, bf16[16,88,1408]{2,1,0:T(8,128)(2,1)S(1)}) custom-call(bf16[264,1408]{1,0:T(8,128)(2,1)S(1)} %fusion.q_own, bf16[88,1408]{1,0:T(8,128)(2,1)S(1)} %fusion.4.p_own), custom_call_target="tpu_custom_call" | custom-call | tf_op jit(solution)/shard_map/gather_weights/pallas_call | solution.py:234
  76.0 4.4 %copy-done = bf16[16,264,1408]{2,1,0:T(8,128)(2,1)} copy-done((bf16[16,264,1408]{2,1,0:T(8,128)(2,1)}, bf16[16,264,1408]{2,1,0:T(8,128)(2,1)S(1)}, u32[]{:S(2)}) %copy-start) | copy-done | bytes 11894808
  80.4 1.9 copy-done.1
  82.3 0.6 broadcast_in_dim.2.gain_ref
  82.9 18.8 %qkv.1.qkv_ref = bf16[2,48,88,257]{3,2,1,0:T(8,128)(2,1)} custom-call(bf16[514,1408]{1,0:T(8,128)(2,1)} %images_ref.3, f32[1,1408]{1,0:T(1,128)} %broadcast_in_dim.2.gain_ref, bf16[4224,1408]{1,0:T(8,128)(2,1)} %bitcast.40), custom_call_target="tpu_custom_call" | custom-call | tf_op jit(solution)/shard_map/qkv/pallas_call | solution.py:288
  101.7 1.4 reduce-window.6
  103.2 0.2 slice_reduce_fusion
  103.4 0.1 bitcast_bitcast_fusion
  103.6 0.6 bitcast_add_fusion.slot_ref
  104.1 23.3 %attend.1 = (bf16[514,1408]{1,0:T(8,128)(2,1)}, bf16[16,34,1408]{2,1,0:T(8,128)(2,1)}) custom-call(bf16[2,48,88,257]{3,2,1,0:T(8,128)(2,1)} %qkv.1.qkv_ref, bf16[1408,1408]{1,0:T(8,128)(2,1)} %bitcast.41, bf16[514,1408]{1,0:T(8,128)(2,1)} %images_ref.3, s32[1,514]{1,0:T(1,128)} %bitcast_add_fusion.slot_ref), custom_call_target="tpu_custom_call" | custom-call | tf_op jit(solution)/shard_map/attend/pallas_call | solution.py:344
  127.4 0.3 fusion.2
  127.8 0.1 reshape.57
  127.9 0.6 pad.9.picks_ref
  128.5 66.1 %exchange.1.rows_ref = bf16[16,34,512]{2,1,0:T(8,128)(2,1)} custom-call(bf16[16,34,1408]{2,1,0:T(8,128)(2,1)} %get-tuple-element.9.rows_ref, bf16[16,16,128]{2,1,0:T(8,128)(2,1)} %pad.9.picks_ref, bf16[1024,1408]{1,0:T(8,128)(2,1)} %captions_ref.1), custom_call_target="tpu_custom_call" | custom-call | tf_op jit(solution)/shard_map/exchange/pallas_call | solution.py:453
  194.7 0.9 copy.28.slot_ref
  195.6 3.8 %give_back.1 = bf16[514,4,128]{2,1,0:T(4,128)(2,1)} custom-call(s32[514,1]{1,0:T(8,128)} %copy.28.slot_ref, bf16[16,34,512]{2,1,0:T(8,128)(2,1)} %exchange.1.rows_ref), custom_call_target="tpu_custom_call" | custom-call | tf_op jit(solution)/shard_map/give_back/pallas_call | solution.py:494
  (20 shorter events, 0.1 us)
Async XLA Ops:
  0.6 1.7 copy-start.2
  2.3 2.0 copy-start.3
  3.1 79.2 %copy-start.5 = (f32[1408]{0:T(1024)S(1)}, f32[1408]{0:T(1024)}, u32[]{:S(2)}) copy-start(f32[1408]{0:T(1024)} %param.10) | copy-start | bytes 16900
  76.0 4.4 %copy-start = (bf16[16,264,1408]{2,1,0:T(8,128)(2,1)}, bf16[16,264,1408]{2,1,0:T(8,128)(2,1)S(1)}, u32[]{:S(2)}) copy-start(bf16[16,264,1408]{2,1,0:T(8,128)(2,1)S(1)} %get-tuple-element.6) | copy-start | bytes 35684356
  80.4 1.9 copy-start.1
  82.9 18.8 %copy-start.4 = (s32[514,1]{0,1:T(1,128)S(1)}, s32[514,1]{0,1:T(1,128)}, u32[]{:S(2)}) copy-start(s32[514,1]{0,1:T(1,128)} %param.16) | copy-start | bytes 6172
  104.1 23.3 %copy-start.6 = (s32[514,4]{0,1:T(4,128)S(1)}, s32[514,4]{0,1:T(4,128)}, u32[]{:S(2)}) copy-start(s32[514,4]{0,1:T(4,128)} %param.17) | copy-start | bytes 24676
where the time goes:
time: 200 us; the launch traced here: 199 us
  Pallas kernels  183 us (92%)
  local copies, waits for them, and re-layouts  9.91 us (5%)
  other arithmetic  4.86 us (2%)
    pallas_call x1, Pallas kernels, gather_call(): pl.pallas_call(gather_kernel, in_specs=[anywhere] * 2, out_specs=(anywher...  71.5 us
    pallas_call x1, Pallas kernels, exchange_call(): pl.pallas_call(exchange_kernel, in_specs=[full] * 3, out_specs=pl.BlockSp...  66.1 us
    pallas_call x1, Pallas kernels, attend_call(): pl.pallas_call(attend_kernel, in_specs=[full] * 4, out_specs=(full, full)...  23.3 us
    pallas_call x1, Pallas kernels, qkv_call(): pl.pallas_call(qkv_kernel, grid=(units // step,), in_specs=[pl.BlockSpec(...  18.8 us
    unnamed x14, local copies, waits for them, and re-layouts  6.37 us

commit v1 on v0

--- a/solution.py
+++ b/solution.py
@@ -36,23 +36,31 @@
 
 
 MESH = pl.DeviceIdType.MESH
-SHARE = 11
-
-
-def gather_kernel(q_own, p_own, q_out, p_out, q_hold, p_hold, rz, ry, rx, rc, sz, sy, sx, sc, held):
-    peers = q_out.shape[0]
+
+def spans_of(rows):
+    third = rows // 24 * 8
+    return (0, rows - 2 * third), (rows - 2 * third, third), (rows - third, third)
+
+
+def front_kernel(
+    images_ref, gain_ref, q_own, p_own, mixed_ref, p_out,
+    q_all, normed, qkv, mixed, rz, ry, rx, rc, sz, sy, sx, sc, held,
+):
+    peers = q_all.shape[0]
     nz = peers // 4
+    group, units, head_dim, patches = qkv.shape
+    lanes = normed.shape[0] // group
+    share = units // peers
     me = lax.axis_index("idx")
     x = lax.axis_index("rep")
     z, y, c = me // 4, (me // 2) % 2, me % 2
-    own, out = (q_own, p_own), (q_out, p_out)
+    own, out = (q_own, p_own), (q_all, p_out)
 
     def at(zz, yy, cc):
         return (zz * 2 + yy) * 2 + cc
 
     to_y, to_c, to_x = (x, at(z, 1 - y, c)), (x, at(z, y, 1 - c)), (1 - x, me)
     to_up, to_down = (x, me + 4), (x, me - 4)
-
     barrier = pltpu.get_barrier_semaphore()
 
     def greet(target):
@@ -73,13 +81,13 @@
     pl.semaphore_wait(barrier, greeted)
 
     def rows(a, k):
-        unit = own[a].shape[0] // SHARE
+        spans = spans_of(own[a].shape[0])
         if k == 0:
-            return pl.ds(0, 3 * unit)
+            return pl.ds(*spans[0])
         if k == 3:
-            return pl.ds(0, SHARE * unit)
+            return pl.ds(0, own[a].shape[0])
         side = x if k == 1 else 1 - x
-        return pl.ds(pl.multiple_of((3 + 4 * side) * unit, 8), 4 * unit)
+        return pl.ds(pl.multiple_of(spans[1][0] + spans[1][1] * side, 8), spans[1][1])
 
     def copy(a, shard, k, mine, send, recv, target):
         span = rows(a, k)
@@ -126,8 +134,7 @@
         def _():
             body(z + distance, 1)
 
-    holds = []
-    for a in range(2):
+    def start_own(a):
         for k in (1, 0):
 
             @pl.when(z + 1 < nz)
@@ -140,58 +147,138 @@
 
             across(a, z, k, y, True).start()
         core(a, z, y, c, 3, True).start()
-        hold = (q_hold, p_hold)[a]
-        load = pltpu.make_async_copy(own[a], hold, held.at[a, 0])
-        load.start()
-        holds.append((load, pltpu.make_async_copy(hold, out[a].at[me], held.at[a, 1])))
-    for load, store in holds:
-        load.wait()
-        store.start()
-
-    for a in range(2):
-        for step in range(1, nz + 2):
-            if step < nz:
-
-                def from_chain(zz, side):
-                    for k in (1, 0):
-                        up(a, zz, k).wait_recv()
-                        if side < 0:
-
-                            @pl.when(z + 1 < nz)
-                            def _():
-                                up(a, zz, k).start()
-                        else:
-
-                            @pl.when(z > 0)
-                            def _():
-                                down(a, zz, k).start()
-
-                        across(a, zz, k, y).start()
-                        if k == 1:
-                            plane(a, zz, y, 1).start()
-                        core(a, zz, y, c, k).start()
-
-                each(step, from_chain)
-            if step <= nz:
-
-                def from_across(zz, side):
-                    for k in (1, 0):
-                        across(a, zz, k, 1 - y).wait_recv()
-                        if k == 1:
-                            plane(a, zz, 1 - y, 1).start()
-                        core(a, zz, 1 - y, c, k).start()
-
-                each(step - 1, from_across)
-            if step >= 2:
-
-                def from_plane(zz, side):
-                    if side != 0:
-                        plane(a, zz, y, 2).wait_recv()
-                        core(a, zz, y, c, 2).start()
-                    plane(a, zz, 1 - y, 2).wait_recv()
-                    core(a, zz, 1 - y, c, 2).start()
-
-                each(step - 2, from_plane)
+        pltpu.make_async_copy(own[a], out[a].at[me], held.at[a]).start()
+
+    def chain_event(a, step):
+        def body(zz, side):
+            for k in (1, 0):
+                up(a, zz, k).wait_recv()
+                if side < 0:
+
+                    @pl.when(z + 1 < nz)
+                    def _():
+                        up(a, zz, k).start()
+                else:
+
+                    @pl.when(z > 0)
+                    def _():
+                        down(a, zz, k).start()
+
+                across(a, zz, k, y).start()
+                if k == 1:
+                    plane(a, zz, y, 1).start()
+                core(a, zz, y, c, k).start()
+
+        each(step, body)
+
+    def across_event(a, distance):
+        def body(zz, side):
+            for k in (1, 0):
+                across(a, zz, k, 1 - y).wait_recv()
+                if k == 1:
+                    plane(a, zz, 1 - y, 1).start()
+                core(a, zz, 1 - y, c, k).start()
+
+        each(distance, body)
+
+    def plane_event(a, distance):
+        def body(zz, side):
+            if side != 0:
+                plane(a, zz, y, 2).wait_recv()
+                core(a, zz, y, c, 2).start()
+            plane(a, zz, 1 - y, 2).wait_recv()
+            core(a, zz, 1 - y, c, 2).start()
+
+        each(distance, body)
+
+    events = dict(chain=chain_event, across=across_event, plane=plane_event, own=lambda a, _: start_own(a))
+
+    def run(listed):
+        for kind, a, distance in listed:
+            events[kind](a, distance)
+
+    def nearest(place):
+        found = z
+        for zz in range(nz):
+            order = sorted(range(nz), key=lambda other: (abs(other - zz), other))
+            for turn in range(nz):
+                hit = jnp.logical_and(z == zz, place == turn)
+                found = jnp.where(hit, order[turn], found)
+        return found
+
+    def settle(a, zz):
+        @pl.when(zz == z)
+        def _():
+            pltpu.make_async_copy(own[a], out[a].at[me], held.at[a]).wait()
+            core(a, z, y, 1 - c, 3).wait_recv()
+            for k in (1, 0, 2):
+                core(a, z, 1 - y, 1 - c, k).wait_recv()
+
+        @pl.when(zz != z)
+        def _():
+            for yy in (y, 1 - y):
+                for k in (1, 0, 2):
+                    core(a, zz, yy, 1 - c, k).wait_recv()
+
+    def qkv_step(turn, _):
+        zz = nearest(turn)
+        for number, listed in enumerate(QKV_EVENTS):
+
+            @pl.when(turn == number)
+            def _():
+                run(listed)
+
+        settle(0, zz)
+
+        def product(part, _):
+            shard = zz * 4 + part
+            every = dot_nt(q_all[shard], normed[...])
+            for g in range(group):
+                found = every[:, g * lanes:g * lanes + patches].reshape(share, head_dim, patches)
+                qkv[g, pl.ds(shard * share, share)] = found.astype(BF16)
+            return 0
+
+        lax.fori_loop(0, 4, product, 0)
+        return 0
+
+    scale = head_dim ** (-0.5)
+    bunch = 4
+    rounds = HEADS // bunch
+
+    def head_step(turn, _):
+        for number, listed in enumerate(HEAD_EVENTS):
+
+            @pl.when(turn == number)
+            def _():
+                run(listed)
+
+        g = turn // rounds
+        for b in range(bunch):
+            h = (turn % rounds) * bunch + b
+            queries, keys, vals = qkv[g, h], qkv[g, HEADS + h], qkv[g, 2 * HEADS + h]
+            logits = lax.dot_general(
+                keys, queries, (((0,), (0,)), ((), ())), preferred_element_type=F32
+            )
+            logits = logits * scale
+            weights = jnp.exp(logits - jnp.max(logits, axis=0, keepdims=True))
+            probs = weights * (1.0 / jnp.sum(weights, axis=0, keepdims=True))
+            found = jnp.dot(vals, probs.astype(BF16), preferred_element_type=F32)
+            mixed[g, pl.ds(pl.multiple_of(h * head_dim, 8), head_dim), :] = found
+        return 0
+
+    start_own(0)
+    normed[...] = jnp.zeros_like(normed)
+    for g in range(group):
+        normed[g * lanes:g * lanes + patches] = layer_norm(
+            images_ref[g * patches:(g + 1) * patches], gain_ref[...]
+        )
+    lax.fori_loop(0, nz, qkv_step, 0)
+    lax.fori_loop(0, group * rounds, head_step, 0)
+    run(LAST_EVENTS)
+    for g in range(group):
+        mixed_ref[g * patches:(g + 1) * patches] = mixed[g].T.astype(BF16)
+    for zz in range(nz):
+        settle(1, zz)
 
     for a in range(2):
         for distance in range(nz):
@@ -215,30 +302,61 @@
                 for yy, mine in ((y, first), (1 - y, False)):
                     if mine:
                         core(a, zz, yy, c, 3, True).wait_send()
-                        core(a, zz, yy, 1 - c, 3).wait_recv()
                         continue
                     plane(a, zz, yy, 1).wait_send()
                     for k in (1, 0, 2):
                         core(a, zz, yy, c, k).wait_send()
-                        core(a, zz, yy, 1 - c, k).wait_recv()
 
             each(distance, finish)
-    for load, store in holds:
-        store.wait()
-
-
-def gather_call(q_own, p_own, peers):
-    anywhere = pl.BlockSpec(memory_space=pl.ANY)
+
+
+QKV_EVENTS = (
+    (("chain", 0, 1), ("own", 1, 0), ("across", 0, 0), ("plane", 0, 0)),
+    (("chain", 0, 2), ("across", 0, 1), ("plane", 0, 1)),
+    (("chain", 0, 3), ("across", 0, 2), ("chain", 1, 1), ("plane", 0, 2)),
+    (("across", 0, 3), ("across", 1, 0), ("chain", 1, 2), ("plane", 0, 3)),
+)
+HEAD_EVENTS = (
+    (("across", 1, 1), ("chain", 1, 3), ("plane", 1, 0)),
+    (("across", 1, 2),),
+    (("plane", 1, 1),),
+    (("across", 1, 3),),
+    (("plane", 1, 2),),
+    (),
+    (),
+    (("plane", 1, 3),),
+)
+LAST_EVENTS = ()
+
+
+def fits(images, q_own, p_own, peers, reps):
+    tokens, width = images.shape
+    rows_whole = all(own.shape[0] % 88 == 0 for own in (q_own, p_own))
+    layout = peers == 4 * len(QKV_EVENTS) and reps == 2
+    return layout and rows_whole and width == peers * p_own.shape[0] and tokens % PATCHES == 0
+
+
+def front_call(images, gain, q_own, p_own, peers):
+    tokens, width = images.shape
+    group = tokens // PATCHES
+    head_dim = width // HEADS
+    lanes = -(-PATCHES // 128) * 128
+    full = pl.BlockSpec(memory_space=VMEM)
     nz = peers // 4
     dma = pltpu.SemaphoreType.DMA
     return pl.pallas_call(
-        gather_kernel,
-        in_specs=[anywhere] * 2,
-        out_specs=(anywhere, anywhere),
-        out_shape=tuple(jax.ShapeDtypeStruct((peers,) + own.shape, own.dtype) for own in (q_own, p_own)),
+        front_kernel,
+        in_specs=[full] * 4,
+        out_specs=(full, pl.BlockSpec(memory_space=pl.ANY)),
+        out_shape=(
+            jax.ShapeDtypeStruct((tokens, width), BF16),
+            jax.ShapeDtypeStruct((peers,) + p_own.shape, BF16),
+        ),
         scratch_shapes=[
-            pltpu.VMEM(q_own.shape, q_own.dtype),
-            pltpu.VMEM(p_own.shape, p_own.dtype),
+            pltpu.VMEM((peers,) + q_own.shape, BF16),
+            pltpu.VMEM((group * lanes, width), BF16),
+            pltpu.VMEM((group, 3 * HEADS, head_dim, PATCHES), BF16),
+            pltpu.VMEM((group, width, PATCHES), F32),
             dma((2, nz, 2)),
             dma((2, nz, 2)),
             dma((2, 2 * nz)),
@@ -247,21 +365,13 @@
             dma((2, nz, 2)),
             dma((2, 2 * nz)),
             dma((2, 2 * nz, 3)),
-            dma((2, 2)),
+            dma((2,)),
         ],
         compiler_params=pltpu.CompilerParams(
-            collective_id=0, has_side_effects=True, vmem_limit_bytes=4 * 1024 * 1024
+            collective_id=0, has_side_effects=True, vmem_limit_bytes=VLIMIT
         ),
-        name="gather_weights",
-    )(q_own, p_own)
-
-
-def gather_rows(q_own, p_own, peers, reps):
-    fits = all(own.shape[0] % (8 * SHARE) == 0 for own in (q_own, p_own))
-    if fits and peers % 8 == 0 and reps == 2:
-        w_qkv, w_proj = gather_call(q_own, p_own, peers)
-        return tuple(w.reshape(-1, w.shape[2]) for w in (w_qkv, w_proj))
-    return tuple(lax.all_gather(own, "idx", axis=0, tiled=True) for own in (q_own, p_own))
+        name="front",
+    )(images, gain, q_own, p_own)
 
 
 def qkv_kernel(images_ref, gain_ref, w_ref, out_ref, normed):
@@ -378,97 +488,260 @@
     )(rows, picks, captions)
 
 
+def capacity_of(tokens, peers):
+    return (tokens + peers - 1) // peers + 1
+
+
+def split_of(tokens, peers):
+    capacity = capacity_of(tokens, peers)
+    return capacity // 8 * 8, capacity % 8
+
+
 def stride_of(capacity):
     return -(-capacity // 8) * 8
 
 
-def exchange_kernel(
-    rows_ref, picks_ref, captions_ref, got_ref,
-    rows_in, picks_in, flat, every, chosen, rs, rr, ps, pr, bs, br, own_sem,
+def back_kernel(
+    mixed_ref, proj_ref, images_ref, slot_ref, picks_ref, captions_ref, emb_ref, out_ref,
+    onehot, rows_out, rows_in, picks_in, chosen, got, columns, rest_columns, emb, total,
+    wide, rest_out, rest_in, tall, tail_out, tail_in,
+    rs, rr, ps, pr, bs, br, es, er, ts, tr, own_sem,
 ):
-    peers, capacity = rows_ref.shape[0], rows_ref.shape[1]
-    stride = flat.shape[0] // peers
-    pick_count = chosen.shape[2] // CAPT
+    peers = picks_ref.shape[0]
+    tokens = slot_ref.shape[1]
+    width = rows_out.shape[1]
+    full, extra = split_of(tokens, peers)
+    base, count = peers * full, peers * extra
+    pick_count = out_ref.shape[1]
+    nz, block = peers // 4, 4 * full
     me = lax.axis_index("idx")
     rep = lax.axis_index("rep")
-
-    def other(step):
-        return (me + step) % peers
-
+    z = me // 4
     barrier = pltpu.get_barrier_semaphore()
     for step in range(1, peers):
-        pl.semaphore_signal(barrier, inc=1, device_id=(rep, other(step)), device_id_type=MESH)
+        pl.semaphore_signal(
+            barrier, inc=1, device_id=(rep, (me + step) % peers), device_id_type=MESH
+        )
+
+    def at(p):
+        return pl.ds(pl.multiple_of(p * full, 8), full)
+
+    def mover(src, dst, sends, recvs, flat):
+        def move(p, home):
+            return pltpu.make_async_remote_copy(
+                src_ref=src.at[at(p) if flat else p],
+                dst_ref=dst.at[at(home) if flat else home],
+                send_sem=sends.at[p],
+                recv_sem=recvs.at[home],
+                device_id=(rep, p),
+                device_id_type=MESH,
+            )
+
+        return move
+
+    def keeper(src, dst, number, flat):
+        here = at(me) if flat else me
+        return pltpu.make_async_copy(src.at[here], dst.at[here], own_sem.at[number])
+
+    moves = (
+        (rows_out, rows_in, rs, rr, True),
+        (picks_ref, picks_in, ps, pr, False),
+        (chosen, got, bs, br, True),
+        (rest_out, rest_in, es, er, False),
+        (tail_out, tail_in, ts, tr, False),
+    )
+    rows_to, picks_to, back_to, rest_to, tail_to = [mover(*m) for m in moves]
+    own_rows, own_picks, own_back, own_rest, own_tail = [
+        keeper(m[0], m[1], number, m[4]) for number, m in enumerate(moves)
+    ]
+    keep = pltpu.make_async_copy(emb, emb_ref, own_sem.at[len(moves)])
+
+    def farthest(place):
+        found = z
+        for zz in range(nz):
+            order = sorted(
+                range(nz), key=lambda other: (-abs(other - zz), (other < nz // 2) == (zz < nz // 2))
+            )
+            for turn in range(nz):
+                found = jnp.where(jnp.logical_and(z == zz, place == turn), order[turn], found)
+        return found
+
+    def each(zz, local, remote):
+        for part in range(4):
+            p = zz * 4 + part
+
+            @pl.when(p == me)
+            def _():
+                local()
+
+            @pl.when(p != me)
+            def _():
+                remote(p)
+
+    def each_plane(body):
+        def step(turn, _):
+            body(farthest(turn))
+            return 0
+
+        lax.fori_loop(0, nz, step, 0)
+
     pl.semaphore_wait(barrier, peers - 1)
-
-    def send(src, dst, send_sems, recv_sems, step):
-        return pltpu.make_async_remote_copy(
-            src_ref=src.at[other(step)],
-            dst_ref=dst.at[me],
-            send_sem=send_sems.at[step],
-            recv_sem=recv_sems.at[step],
-            device_id=(rep, other(step)),
-            device_id_type=MESH,
+    own_picks.start()
+    for step in range(1, peers):
+        picks_to((me + step) % peers, me).start()
+
+    def embed(start, size):
+        here = pl.ds(start, size)
+        pick = lax.broadcasted_iota(jnp.int32, (size, tokens), 0) == slot_ref[...] - start
+        onehot[here, :] = jnp.where(pick, 1.0, 0.0).astype(BF16)
+        mine = onehot[here, :]
+        left = jnp.dot(mine, mixed_ref[...], preferred_element_type=F32).astype(BF16)
+        hidden = jnp.dot(mine, images_ref[...], preferred_element_type=F32) + dot_nt(left, proj_ref[...])
+        inv_scale = lax.rsqrt(jnp.mean(hidden * hidden, axis=-1, keepdims=True) + 1e-06)
+        return hidden * inv_scale
+
+    def project(zz):
+        start = pl.multiple_of(zz * block, block)
+        rows_out[pl.ds(start, block), :] = embed(start, block).astype(BF16)
+        each(zz, own_rows.start, lambda p: rows_to(p, me).start())
+
+    each_plane(project)
+    rest = embed(base, count)
+    rows_out[base:base + count, :] = rest.astype(BF16)
+    wide[...] = jnp.zeros_like(wide)
+    tiles = width // 128
+    for e in range(extra):
+        for t in range(tiles):
+            u = e * tiles + t
+            wide[:, u % 8, u // 8 * 128:u // 8 * 128 + 128] = rest[
+                e * peers:(e + 1) * peers, t * 128:(t + 1) * 128
+            ]
+    rest_out[...] = wide[...].astype(BF16)
+    each_plane(lambda zz: each(zz, own_rest.start, lambda p: rest_to(p, me).start()))
+    emb[...] = lax.dot_general(
+        onehot[...], rows_out[...], (((0,), (0,)), ((), ())), preferred_element_type=F32
+    ).astype(BF16)
+    keep.start()
+
+    def chosen_of(every, picks, k):
+        pick = picks[:, k:k + 1]
+        best = jnp.zeros((every.shape[0], CAPT), F32)
+        for b in range(CBLK):
+            best = jnp.where(pick == float(b), every[:, b * CAPT:(b + 1) * CAPT], best)
+        return best
+
+    def score(zz):
+        here = pl.ds(pl.multiple_of(zz * block, block), block)
+
+        def landed(p):
+            picks_to(p, p).wait_recv()
+            rows_to(p, p).wait_recv()
+
+        def kept():
+            own_picks.wait()
+            own_rows.wait()
+
+        each(zz, kept, landed)
+        for part in range(4):
+            p = zz * 4 + part
+            turned = picks_in[p].astype(F32).T
+            columns[part * full:(part + 1) * full] = turned[:full, :]
+            for e in range(extra):
+                rest_columns[pl.ds(e * peers + p, 1), :] = turned[full + e:full + e + 1, :]
+        every = dot_nt(rows_in[here, :], captions_ref[...])
+        for k in range(pick_count):
+            chosen[here, k * CAPT:(k + 1) * CAPT] = chosen_of(every, columns, k).astype(BF16)
+        each(zz, own_back.start, lambda p: back_to(p, me).start())
+
+    each_plane(score)
+    each_plane(lambda zz: each(zz, own_rest.wait, lambda p: rest_to(p, p).wait_recv()))
+    wide[...] = rest_in[...].astype(F32)
+    for e in range(extra):
+        for t in range(tiles):
+            u = e * tiles + t
+            part = wide[:, u % 8, u // 8 * 128:u // 8 * 128 + 128]
+            rows_in[base + e * peers:base + (e + 1) * peers, t * 128:(t + 1) * 128] = part.astype(BF16)
+    every = dot_nt(rows_in[base:base + count, :], captions_ref[...])
+    tall[...] = jnp.zeros_like(tall)
+    for k in range(pick_count):
+        best = chosen_of(every, rest_columns, k)
+        for e in range(extra):
+            tall[:, e * pick_count + k, :] = best[e * peers:(e + 1) * peers]
+    tail_out[...] = tall[...].astype(BF16)
+    each_plane(lambda zz: each(zz, own_tail.start, lambda p: tail_to(p, me).start()))
+    total[...] = jnp.zeros_like(total)
+
+    def give(here):
+        total[...] += lax.dot_general(
+            onehot[here, :], got[here, :], (((0,), (0,)), ((), ())), preferred_element_type=F32
         )
 
-    order = sorted(range(1, peers), key=lambda step: -min(step, peers - step))
-    for step in order:
-        send(rows_ref, rows_in, rs, rr, step).start()
-    for step in order:
-        send(picks_ref, picks_in, ps, pr, step).start()
-    own_rows = pltpu.make_async_copy(rows_ref.at[me], rows_in.at[me], own_sem.at[0])
-    own_picks = pltpu.make_async_copy(picks_ref.at[me], picks_in.at[me], own_sem.at[1])
-    own_rows.start()
-    own_picks.start()
-    own_rows.wait()
-    own_picks.wait()
-    for step in order:
-        send(rows_ref, rows_in, rs, rr, step).wait()
-        send(picks_ref, picks_in, ps, pr, step).wait()
-    for p in range(peers):
-        flat[p * stride:p * stride + capacity, :] = rows_in[p]
-    every[...] = dot_nt(flat[...], captions_ref[...])
-    for p in range(peers):
-        columns = picks_in[p].astype(F32).T
-        span = slice(p * stride, p * stride + capacity)
-        for k in range(pick_count):
-            pick = columns[:capacity, k:k + 1]
-            best = jnp.zeros((capacity, CAPT), F32)
-            for b in range(CBLK):
-                best = jnp.where(pick == float(b), every[span, b * CAPT:(b + 1) * CAPT], best)
-            chosen[p, :, k * CAPT:(k + 1) * CAPT] = best.astype(BF16)
-    for step in order:
-        send(chosen, got_ref, bs, br, step).start()
-    own_back = pltpu.make_async_copy(chosen.at[me], got_ref.at[me], own_sem.at[2])
-    own_back.start()
-    own_back.wait()
-    for step in order:
-        send(chosen, got_ref, bs, br, step).wait()
-
-
-def exchange_call(rows, picks, captions, pick_count):
-    peers, capacity, width = rows.shape
+    def take(zz):
+        each(zz, own_back.wait, lambda p: back_to(p, p).wait_recv())
+        give(pl.ds(pl.multiple_of(zz * block, block), block))
+
+    each_plane(take)
+    each_plane(lambda zz: each(zz, own_tail.wait, lambda p: tail_to(p, p).wait_recv()))
+    tall[...] = tail_in[...].astype(F32)
+    for k in range(pick_count):
+        for e in range(extra):
+            got[base + e * peers:base + (e + 1) * peers, k * CAPT:(k + 1) * CAPT] = tall[
+                :, e * pick_count + k, :
+            ].astype(BF16)
+    give(pl.ds(base, count))
+    for k in range(pick_count):
+        out_ref[:, k, :] = total[:, k * CAPT:(k + 1) * CAPT].astype(BF16)
+    keep.wait()
+
+    def sent(p):
+        for move in (rows_to, picks_to, back_to, rest_to, tail_to):
+            move(p, me).wait_send()
+
+    each_plane(lambda zz: each(zz, lambda: None, sent))
+
+
+def back_call(mixed, w_proj, images, slot_row, picks, captions, pick_count):
+    tokens, width = images.shape
+    peers = picks.shape[0]
+    full_rows, extra = split_of(tokens, peers)
+    slots = peers * (full_rows + extra)
+    rest_shape = (peers, 8, -(-extra * (width // 128) // 8) * 128)
+    tail_shape = (peers, -(-extra * pick_count // 8) * 8, CAPT)
     full = pl.BlockSpec(memory_space=VMEM)
-    flat = peers * stride_of(capacity)
     dma = pltpu.SemaphoreType.DMA
     return pl.pallas_call(
-        exchange_kernel,
-        in_specs=[full] * 3,
-        out_specs=pl.BlockSpec(memory_space=pl.ANY),
-        out_shape=jax.ShapeDtypeStruct((peers, capacity, pick_count * CAPT), BF16),
+        back_kernel,
+        in_specs=[full] * 6,
+        out_specs=(pl.BlockSpec(memory_space=pl.ANY), full),
+        out_shape=(
+            jax.ShapeDtypeStruct((tokens, width), BF16),
+            jax.ShapeDtypeStruct((tokens, pick_count, CAPT), BF16),
+        ),
         scratch_shapes=[
-            pltpu.VMEM(rows.shape, BF16),
-            pltpu.VMEM(picks.shape, BF16),
-            pltpu.VMEM((flat, width), BF16),
-            pltpu.VMEM((flat, captions.shape[0]), F32),
-            pltpu.VMEM((peers, capacity, pick_count * CAPT), BF16),
+            VMEM((slots, tokens), BF16),
+            VMEM((slots, width), BF16),
+            VMEM((slots, width), BF16),
+            VMEM(picks.shape, BF16),
+            VMEM((slots, pick_count * CAPT), BF16),
+            VMEM((slots, pick_count * CAPT), BF16),
+            VMEM((4 * full_rows, picks.shape[1]), F32),
+            VMEM((peers * extra, picks.shape[1]), F32),
+            VMEM((tokens, width), BF16),
+            VMEM((tokens, pick_count * CAPT), F32),
+            VMEM(rest_shape, F32),
+            VMEM(rest_shape, BF16),
+            VMEM(rest_shape, BF16),
+            VMEM(tail_shape, F32),
+            VMEM(tail_shape, BF16),
+            VMEM(tail_shape, BF16),
         ]
-        + [dma((peers,))] * 6
-        + [dma((3,))],
+        + [dma((peers,))] * 10
+        + [dma((6,))],
         compiler_params=pltpu.CompilerParams(
             collective_id=1, has_side_effects=True, vmem_limit_bytes=VLIMIT
         ),
-        name="exchange",
-    )(rows, picks, captions)
+        name="back",
+    )(mixed, w_proj, images, slot_row, picks, captions)
 
 
 def return_kernel(slot_ref, rows_ref, out_ref, *packed):
@@ -518,7 +791,7 @@
     token_count, width = images.shape
     peer_count = lax.axis_size("idx")
     me = lax.axis_index("idx")
-    capacity = (token_count + peer_count - 1) // peer_count + 1
+    capacity = capacity_of(token_count, peer_count)
 
     def own_exponents(exponents, cols):
         return lax.dynamic_slice_in_dim(exponents, me * cols, cols, axis=1)
@@ -526,39 +799,44 @@
     qkv_cols, proj_cols = qkv_values.shape[1], proj_values.shape[1]
     qkv_own = dequant_rows(qkv_values, own_exponents(qkv_exponents, qkv_cols))
     proj_own = dequant_rows(proj_values, own_exponents(proj_exponents, proj_cols))
-    w_qkv, w_proj = gather_rows(qkv_own, proj_own, peer_count, lax.axis_size("rep"))
+    joined = fits(images, qkv_own, proj_own, peer_count, lax.axis_size("rep"))
 
     owner_ids = owners[:, 0]
     onehot = (owner_ids[:, None] == jnp.arange(peer_count, dtype=jnp.int32)[None, :]).astype(
         jnp.int32
     )
     slot_rank = jnp.sum((jnp.cumsum(onehot, axis=0) - onehot) * onehot, axis=1)
-    slot_index = owner_ids * capacity + slot_rank
-    slots = peer_count * capacity
+    stride = stride_of(capacity) if joined else capacity
+    slot_index = owner_ids * stride + slot_rank
+    slots = peer_count * stride
     pick_count = candidates.shape[1]
     dispatch = (jnp.arange(slots, dtype=jnp.int32)[:, None] == slot_index[None, :]).astype(BF16)
     send_picks = jnp.dot(dispatch, candidates.astype(BF16), preferred_element_type=F32).astype(BF16)
-    qkv = qkv_call(images, norm_gain[None, :], w_qkv)
-    if capacity >= 16:
-        turned = send_picks.reshape(peer_count, capacity, pick_count).transpose(0, 2, 1)
-        turned = jnp.pad(turned, ((0, 0), (0, 16 - pick_count), (0, 128 - capacity)))
-        embedding, send_rows = attend_call(
-            qkv, w_proj, images, slot_index[None, :], (peer_count, capacity)
+    gain = norm_gain[None, :]
+    if joined:
+        turned = send_picks.reshape(peer_count, stride, pick_count).transpose(0, 2, 1)
+        turned = jnp.pad(turned, ((0, 0), (0, 8 - pick_count), (0, 128 - stride)))
+        whole, _ = split_of(token_count, peer_count)
+        place = jnp.where(
+            slot_rank < whole,
+            owner_ids * whole + slot_rank,
+            peer_count * slot_rank + owner_ids,
         )
-        returned = exchange_call(send_rows, turned, captions, pick_count)
-        place = owner_ids * stride_of(capacity) + slot_rank
-    else:
-        embedding, send_rows = attend_call(qkv, w_proj, images, slot_index[None, :], (slots,))
-
-        def swap(blocks):
-            shaped = blocks.reshape(peer_count, capacity, blocks.shape[1])
-            moved = lax.all_to_all(shaped, "idx", split_axis=0, concat_axis=0, tiled=True)
-            return moved.reshape(blocks.shape)
-
-        returned = swap(score_call(swap(send_rows), swap(send_picks), captions))
-        place = slot_index
-    scores = return_call(place[:, None], returned, pick_count)
-    return (embedding, scores)
+        mixed, w_proj = front_call(images, gain, qkv_own, proj_own, peer_count)
+        return back_call(
+            mixed, w_proj.reshape(width, width), images, place[None, :], turned, captions, pick_count
+        )
+    w_qkv, w_proj = (lax.all_gather(own, "idx", axis=0, tiled=True) for own in (qkv_own, proj_own))
+    qkv = qkv_call(images, gain, w_qkv)
+    embedding, send_rows = attend_call(qkv, w_proj, images, slot_index[None, :], (slots,))
+
+    def swap(blocks):
+        shaped = blocks.reshape(peer_count, capacity, blocks.shape[1])
+        moved = lax.all_to_all(shaped, "idx", split_axis=0, concat_axis=0, tiled=True)
+        return moved.reshape(blocks.shape)
+
+    returned = swap(score_call(swap(send_rows), swap(send_picks), captions))
+    return (embedding, return_call(slot_index[:, None], returned, pick_count))
 
 
 def solution(mesh):

time: 200 us -> 171 us (0.85)
  Pallas kernels: 183 us -> 154 us
  local copies, waits for them, and re-layouts: 9.91 us -> 6.79 us
  other arithmetic: 4.86 us -> 7.49 us
    pallas_call x5 -> x2, Pallas kernels: 183 us -> 154 us  [the longest x1 93.1 us: front_call(): pl.pallas_call(front_kernel, in_specs=[full] * 4, out_specs=(full, pl.Blo...]
    unnamed x14 -> x8, local copies, waits for them, and re-layouts: 6.37 us -> 3.45 us
where the time goes in v1:
time: 171 us; the launch traced here: 170 us
  Pallas kernels  154 us (90%)
  other arithmetic  7.49 us (4%)
  local copies, waits for them, and re-layouts  6.79 us (4%)
    pallas_call x1, Pallas kernels, front_call(): pl.pallas_call(front_kernel, in_specs=[full] * 4, out_specs=(full, pl.Blo...  93.1 us
    pallas_call x1, Pallas kernels, back_call(): pl.pallas_call(back_kernel, in_specs=[full] * 6, out_specs=(pl.BlockSpec(...  61.3 us
    unnamed x8, local copies, waits for them, and re-layouts  3.45 us

profile of v1, /device:TPU:0, one launch (start us, length us, event | category | flops | bytes accessed | tf_op | source)
XLA Modules:
  0.0 170.5 jit_solution(14515669969492567842)
XLA Ops:
  0.6 0.0 copy-start.2
  0.6 0.7 reduce
  1.4 1.3 broadcast_in_dim.2.gain_ref
  2.7 0.8 exponential_bitcast_fusion.1
  3.5 0.8 exponential_bitcast_fusion
  4.4 1.4 reduce-window.6
  5.8 0.2 slice_reduce_fusion
  6.1 0.1 bitcast_bitcast_fusion
  6.2 1.3 compare_select_fusion.slot_ref
  7.5 1.1 fusion.2
  8.5 0.1 reshape.75
  8.7 0.6 pad.9.picks_ref
  9.3 0.1 copy.14
  9.4 0.1 copy.13
  9.5 0.3 mul.69
  9.8 0.0 copy-start
  9.8 0.9 fusion.4.p_own
  10.6 0.6 mul.65
  11.2 0.0 copy-done
  11.3 1.4 fusion.1.q_own
  12.7 93.1 %front.1 = (bf16[514,1408]{1,0:T(8,128)(2,1)}, bf16[16,88,1408]{2,1,0:T(8,128)(2,1)}) custom-call(bf16[514,1408]{1,0:T(8,128)(2,1)} %images_ref.3, f32[1,1408]{1,0:T(1,128)} %broadcast_in_dim.2.gain_ref, bf16[264,1408]{1,0:T(8,128)(2,1)} %fusion.1.q_own, bf16[88,1408]{1,0:T(8,128)(2,1)} %fusion.4.p_own), custom_call_target="tpu_custom_call" | custom-call | tf_op jit(solution)/shard_map/front/pallas_call | solution.py:347
  105.8 61.3 %back.1 = (bf16[514,1408]{1,0:T(8,128)(2,1)}, bf16[514,4,128]{2,1,0:T(4,128)(2,1)}) custom-call(bf16[514,1408]{1,0:T(8,128)(2,1)} %get-tuple-element.4.mixed_ref, bf16[1408,1408]{1,0:T(8,128)(2,1)} %bitcast.47, bf16[514,1408]{1,0:T(8,128)(2,1)} %images_ref.3, s32[1,514]{1,0:T(1,128)} %compare_select_fusion.slot_ref, bf16[16,8,128]{2,1,0:T(8,128)(2,1)} %pad.9.picks_ref, ...), custom_call_target="tpu_custom_call" | custom-call | tf_op jit(solution)/shard_map/back/pallas_call | solution.py:712
  167.0 2.6 %copy.30 = bf16[514,1408]{1,0:T(8,128)(2,1)} copy(bf16[514,1408]{1,0:T(8,128)(2,1)} %get-tuple-element.8) | data formatting | bytes 2894848
  169.7 0.8 copy.31
  (9 shorter events, 0.1 us)
Async XLA Ops:
  0.6 9.1 %copy-start.2 = (bf16[1408,88]{0,1:T(8,128)(2,1)S(1)}, bf16[1408,88]{0,1:T(8,128)(2,1)}, u32[]{:S(2)}) copy-start(bf16[1408,88]{0,1:T(8,128)(2,1)} %param.13) | copy-start | bytes 743428
  9.8 1.5 copy-start
  167.0 2.7 %copy-start.1 = (bf16[514,4,128]{2,1,0:T(4,128)(2,1)S(1)}, bf16[514,4,128]{2,1,0:T(4,128)(2,1)}, u32[]{:S(2)}) copy-start(bf16[514,4,128]{2,1,0:T(4,128)(2,1)} %get-tuple-element.9) | copy-start | bytes 1579012

commit v2 on v1

--- a/solution.py
+++ b/solution.py
@@ -36,6 +36,10 @@
 
 
 MESH = pl.DeviceIdType.MESH
+
+FRONT_LIMIT = 38 * 1024 * 1024
+BACK_LIMIT = 40 * 1024 * 1024
+
 
 def spans_of(rows):
     third = rows // 24 * 8
@@ -149,9 +153,9 @@
         core(a, z, y, c, 3, True).start()
         pltpu.make_async_copy(own[a], out[a].at[me], held.at[a]).start()
 
-    def chain_event(a, step):
+    def chain_event(a, step, kinds):
         def body(zz, side):
-            for k in (1, 0):
+            for k in kinds:
                 up(a, zz, k).wait_recv()
                 if side < 0:
 
@@ -171,9 +175,9 @@
 
         each(step, body)
 
-    def across_event(a, distance):
+    def across_event(a, distance, kinds):
         def body(zz, side):
-            for k in (1, 0):
+            for k in kinds:
                 across(a, zz, k, 1 - y).wait_recv()
                 if k == 1:
                     plane(a, zz, 1 - y, 1).start()
@@ -191,11 +195,19 @@
 
         each(distance, body)
 
-    events = dict(chain=chain_event, across=across_event, plane=plane_event, own=lambda a, _: start_own(a))
-
     def run(listed):
-        for kind, a, distance in listed:
-            events[kind](a, distance)
+        for event in listed:
+            a = int(event[-1] if event[0] == "o" else event[1])
+            if event[0] == "o":
+                start_own(a)
+                continue
+            distance, kinds = int(event[2]), tuple(int(k) for k in event[3:])
+            if event[0] == "c":
+                chain_event(a, distance, kinds)
+            elif event[0] == "x":
+                across_event(a, distance, kinds)
+            else:
+                plane_event(a, distance)
 
     def nearest(place):
         found = z
@@ -221,24 +233,23 @@
                     core(a, zz, yy, 1 - c, k).wait_recv()
 
     def qkv_step(turn, _):
-        zz = nearest(turn)
+        zz = nearest(turn // 4)
         for number, listed in enumerate(QKV_EVENTS):
-
-            @pl.when(turn == number)
-            def _():
-                run(listed)
-
-        settle(0, zz)
-
-        def product(part, _):
-            shard = zz * 4 + part
-            every = dot_nt(q_all[shard], normed[...])
-            for g in range(group):
-                found = every[:, g * lanes:g * lanes + patches].reshape(share, head_dim, patches)
-                qkv[g, pl.ds(shard * share, share)] = found.astype(BF16)
-            return 0
-
-        lax.fori_loop(0, 4, product, 0)
+            if listed:
+
+                @pl.when(turn == number)
+                def _():
+                    run(listed)
+
+        @pl.when(turn % 4 == 0)
+        def _():
+            settle(0, zz)
+
+        shard = zz * 4 + turn % 4
+        every = dot_nt(q_all[shard], normed[...])
+        for g in range(group):
+            found = every[:, g * lanes:g * lanes + patches].reshape(share, head_dim, patches)
+            qkv[g, pl.ds(shard * share, share)] = found.astype(BF16)
         return 0
 
     scale = head_dim ** (-0.5)
@@ -247,10 +258,11 @@
 
     def head_step(turn, _):
         for number, listed in enumerate(HEAD_EVENTS):
-
-            @pl.when(turn == number)
-            def _():
-                run(listed)
+            if listed:
+
+                @pl.when(turn == number)
+                def _():
+                    run(listed)
 
         g = turn // rounds
         for b in range(bunch):
@@ -263,20 +275,24 @@
             weights = jnp.exp(logits - jnp.max(logits, axis=0, keepdims=True))
             probs = weights * (1.0 / jnp.sum(weights, axis=0, keepdims=True))
             found = jnp.dot(vals, probs.astype(BF16), preferred_element_type=F32)
-            mixed[g, pl.ds(pl.multiple_of(h * head_dim, 8), head_dim), :] = found
+            mixed[pl.ds(pl.multiple_of(h * head_dim, 8), head_dim), :] = found
+        for image in range(group):
+
+            @pl.when(turn == image * rounds + rounds - 1)
+            def _():
+                mixed_ref[image * patches:(image + 1) * patches] = mixed[...].T.astype(BF16)
+
         return 0
 
-    start_own(0)
+    run(LEAD_EVENTS)
     normed[...] = jnp.zeros_like(normed)
     for g in range(group):
         normed[g * lanes:g * lanes + patches] = layer_norm(
             images_ref[g * patches:(g + 1) * patches], gain_ref[...]
         )
-    lax.fori_loop(0, nz, qkv_step, 0)
+    lax.fori_loop(0, len(QKV_EVENTS), qkv_step, 0)
     lax.fori_loop(0, group * rounds, head_step, 0)
     run(LAST_EVENTS)
-    for g in range(group):
-        mixed_ref[g * patches:(g + 1) * patches] = mixed[g].T.astype(BF16)
     for zz in range(nz):
         settle(1, zz)
 
@@ -310,21 +326,34 @@
             each(distance, finish)
 
 
+LEAD_EVENTS = ("own0", "x001", "c011",)
 QKV_EVENTS = (
-    (("chain", 0, 1), ("own", 1, 0), ("across", 0, 0), ("plane", 0, 0)),
-    (("chain", 0, 2), ("across", 0, 1), ("plane", 0, 1)),
-    (("chain", 0, 3), ("across", 0, 2), ("chain", 1, 1), ("plane", 0, 2)),
-    (("across", 0, 3), ("across", 1, 0), ("chain", 1, 2), ("plane", 0, 3)),
+    ("x000", "c010", "x011", "p00", "c021", "c020",),
+    (),
+    ("c031",),
+    ("own1", "x010",),
+    ("p01", "x021",),
+    (),
+    ("c030", "x031", "c111",),
+    ("x020",),
+    ("p02", "c121", "x101",),
+    ("c110", "p03",),
+    ("x030",),
+    (),
+    (),
+    ("c131",),
+    ("c120",),
+    (),
 )
 HEAD_EVENTS = (
-    (("across", 1, 1), ("chain", 1, 3), ("plane", 1, 0)),
-    (("across", 1, 2),),
-    (("plane", 1, 1),),
-    (("across", 1, 3),),
-    (("plane", 1, 2),),
+    (),
+    ("c130",),
+    ("p10", "x121", "x131", "x111",),
     (),
     (),
-    (("plane", 1, 3),),
+    ("p13", "x120", "p12",),
+    ("p11", "x100", "x110", "x130",),
+    (),
 )
 LAST_EVENTS = ()
 
@@ -332,7 +361,7 @@
 def fits(images, q_own, p_own, peers, reps):
     tokens, width = images.shape
     rows_whole = all(own.shape[0] % 88 == 0 for own in (q_own, p_own))
-    layout = peers == 4 * len(QKV_EVENTS) and reps == 2
+    layout = peers == len(QKV_EVENTS) and reps == 2
     return layout and rows_whole and width == peers * p_own.shape[0] and tokens % PATCHES == 0
 
 
@@ -356,7 +385,7 @@
             pltpu.VMEM((peers,) + q_own.shape, BF16),
             pltpu.VMEM((group * lanes, width), BF16),
             pltpu.VMEM((group, 3 * HEADS, head_dim, PATCHES), BF16),
-            pltpu.VMEM((group, width, PATCHES), F32),
+            pltpu.VMEM((width, PATCHES), F32),
             dma((2, nz, 2)),
             dma((2, nz, 2)),
             dma((2, 2 * nz)),
@@ -368,7 +397,7 @@
             dma((2,)),
         ],
         compiler_params=pltpu.CompilerParams(
-            collective_id=0, has_side_effects=True, vmem_limit_bytes=VLIMIT
+            collective_id=0, has_side_effects=True, vmem_limit_bytes=FRONT_LIMIT
         ),
         name="front",
     )(images, gain, q_own, p_own)
@@ -502,7 +531,8 @@
 
 
 def back_kernel(
-    mixed_ref, proj_ref, images_ref, slot_ref, picks_ref, captions_ref, emb_ref, out_ref,
+    mixed_far, proj_far, images_far, slot_ref, picks_ref, captions_far, emb_ref, out_ref,
+    mixed_ref, proj_ref, images_ref, captions_ref, loads,
     onehot, rows_out, rows_in, picks_in, chosen, got, columns, rest_columns, emb, total,
     wide, rest_out, rest_in, tall, tail_out, tail_in,
     rs, rr, ps, pr, bs, br, es, er, ts, tr, own_sem,
@@ -523,6 +553,11 @@
             barrier, inc=1, device_id=(rep, (me + step) % peers), device_id_type=MESH
         )
 
+    ends = ((mixed_far, mixed_ref), (images_far, images_ref), (proj_far, proj_ref), (captions_far, captions_ref))
+    fetched = [pltpu.make_async_copy(*end, loads.at[number]) for number, end in enumerate(ends)]
+    for fetch in fetched:
+        fetch.start()
+
     def at(p):
         return pl.ds(pl.multiple_of(p * full, 8), full)
 
@@ -589,6 +624,9 @@
     own_picks.start()
     for step in range(1, peers):
         picks_to((me + step) % peers, me).start()
+
+    for fetch in fetched[:3]:
+        fetch.wait()
 
     def embed(start, size):
         here = pl.ds(start, size)
@@ -653,6 +691,7 @@
             chosen[here, k * CAPT:(k + 1) * CAPT] = chosen_of(every, columns, k).astype(BF16)
         each(zz, own_back.start, lambda p: back_to(p, me).start())
 
+    fetched[3].wait()
     each_plane(score)
     each_plane(lambda zz: each(zz, own_rest.wait, lambda p: rest_to(p, p).wait_recv()))
     wide[...] = rest_in[...].astype(F32)
@@ -707,17 +746,23 @@
     slots = peers * (full_rows + extra)
     rest_shape = (peers, 8, -(-extra * (width // 128) // 8) * 128)
     tail_shape = (peers, -(-extra * pick_count // 8) * 8, CAPT)
+    anywhere = pl.BlockSpec(memory_space=pl.ANY)
     full = pl.BlockSpec(memory_space=VMEM)
     dma = pltpu.SemaphoreType.DMA
     return pl.pallas_call(
         back_kernel,
-        in_specs=[full] * 6,
-        out_specs=(pl.BlockSpec(memory_space=pl.ANY), full),
+        in_specs=[anywhere] * 3 + [full] * 2 + [anywhere],
+        out_specs=(anywhere, full),
         out_shape=(
             jax.ShapeDtypeStruct((tokens, width), BF16),
             jax.ShapeDtypeStruct((tokens, pick_count, CAPT), BF16),
         ),
         scratch_shapes=[
+            VMEM(mixed.shape, BF16),
+            VMEM(w_proj.shape, BF16),
+            VMEM(images.shape, BF16),
+            VMEM(captions.shape, BF16),
+            dma((4,)),
             VMEM((slots, tokens), BF16),
             VMEM((slots, width), BF16),
             VMEM((slots, width), BF16),
@@ -738,7 +783,7 @@
         + [dma((peers,))] * 10
         + [dma((6,))],
         compiler_params=pltpu.CompilerParams(
-            collective_id=1, has_side_effects=True, vmem_limit_bytes=VLIMIT
+            collective_id=1, has_side_effects=True, vmem_limit_bytes=BACK_LIMIT
         ),
         name="back",
     )(mixed, w_proj, images, slot_row, picks, captions)

time: 171 us -> 145 us (0.85)
  Pallas kernels: 154 us -> 132 us
  other arithmetic: 7.49 us -> 5.56 us
  local copies, waits for them, and re-layouts: 6.79 us -> 5.02 us
    pallas_call x1, Pallas kernels: 93.1 us -> 76.1 us  [front_call(): pl.pallas_call(front_kernel, in_specs=[full] * 4, out_specs=(full, pl.Blo...]
    pallas_call x1, Pallas kernels: 61.3 us -> 56.3 us  [back_call(): pl.pallas_call(back_kernel, in_specs=[anywhere] * 3 + [full] * 2 + [anywh...]
    unnamed x8 -> x10, local copies, waits for them, and re-layouts: 3.45 us -> 2.87 us
where the time goes in v2:
time: 145 us
  Pallas kernels  132 us (91%)
  other arithmetic  5.56 us (4%)
  local copies, waits for them, and re-layouts  5.02 us (3%)
    pallas_call x1, Pallas kernels, front_call(): pl.pallas_call(front_kernel, in_specs=[full] * 4, out_specs=(full, pl.Blo...  76.1 us
    pallas_call x1, Pallas kernels, back_call(): pl.pallas_call(back_kernel, in_specs=[anywhere] * 3 + [full] * 2 + [anywh...  56.3 us

profile of v2, /device:TPU:0, one launch (start us, length us, event | category | flops | bytes accessed | tf_op | source)
XLA Modules:
  0.0 144.8 jit_solution(5246499768179741698)
XLA Ops:
  0.6 0.0 copy-start.3
  0.6 0.7 reduce
  1.4 0.7 broadcast_in_dim.2.gain_ref
  2.1 0.8 exponential_bitcast_fusion.1
  2.9 0.8 exponential_bitcast_fusion
  3.8 1.4 reduce-window.6
  5.2 0.2 slice_reduce_fusion
  5.5 0.1 bitcast_bitcast_fusion
  5.6 0.7 compare_select_fusion.slot_ref
  6.3 1.1 fusion.2
  7.4 0.1 reshape.75
  7.5 0.1 copy.14
  7.6 0.1 copy.13
  7.7 0.3 mul.69
  8.0 0.0 copy-start.2
  8.0 0.2 fusion.4.p_own
  8.2 0.6 mul.65
  8.8 0.3 copy-done.2
  9.1 0.7 fusion.1.q_own
  9.8 0.6 copy-done
  10.5 76.1 %front.1 = (bf16[514,1408]{1,0:T(8,128)(2,1)S(1)}, bf16[16,88,1408]{2,1,0:T(8,128)(2,1)S(1)}) custom-call(bf16[514,1408]{1,0:T(8,128)(2,1)S(1)} %copy-done, f32[1,1408]{1,0:T(1,128)S(1)} %broadcast_in_dim.2.gain_ref, bf16[264,1408]{1,0:T(8,128)(2,1)S(1)} %fusion.1.q_own, bf16[88,1408]{1,0:T(8,128)(2,1)S(1)} %fusion.4.p_own), custom_call_target="tpu_custom_call" | custom-call | tf_op jit(solution)/shard_map/front/pallas_call | solution.py:376
  86.6 56.3 %back.1 = (bf16[514,1408]{1,0:T(8,128)(2,1)S(1)}, bf16[514,4,128]{2,1,0:T(4,128)(2,1)S(1)}) custom-call(bf16[514,1408]{1,0:T(8,128)(2,1)S(1)} %get-tuple-element.4.mixed_far, bf16[1408,1408]{1,0:T(8,128)(2,1)S(1)} %bitcast.46, bf16[514,1408]{1,0:T(8,128)(2,1)S(1)} %copy-done, s32[1,514]{1,0:T(1,128)S(1)} %compare_select_fusion.slot_ref, ...), custom_call_target="tpu_custom_call" | custom-call | tf_op jit(solution)/shard_map/back/pallas_call | solution.py:752
  142.9 1.1 copy.30
  144.0 0.8 copy.31
  (11 shorter events, 0.1 us)
Async XLA Ops:
  0.6 7.4 %copy-start.3 = (bf16[1408,88]{0,1:T(8,128)(2,1)S(1)}, bf16[1408,88]{0,1:T(8,128)(2,1)}, u32[]{:S(2)}) copy-start(bf16[1408,88]{0,1:T(8,128)(2,1)} %param.13) | copy-start | bytes 743428
  8.0 1.1 copy-start.2
  9.1 1.4 copy-start
  9.1 77.5 %copy-start.1 = (bf16[1024,1408]{1,0:T(8,128)(2,1)S(1)}, bf16[1024,1408]{1,0:T(8,128)(2,1)}, u32[]{:S(2)}) copy-start(bf16[1024,1408]{1,0:T(8,128)(2,1)} %captions_far.1) | copy-start | bytes 8650756

commit v3 on v2

--- a/solution.py
+++ b/solution.py
@@ -37,8 +37,8 @@
 
 MESH = pl.DeviceIdType.MESH
 
-FRONT_LIMIT = 38 * 1024 * 1024
-BACK_LIMIT = 40 * 1024 * 1024
+FRONT_LIMIT = 66_800_000
+BACK_LIMIT = 64_600_000
 
 
 def spans_of(rows):
@@ -46,8 +46,64 @@
     return (0, rows - 2 * third), (rows - 2 * third, third), (rows - third, third)
 
 
+def powers_of_two(exponents):
+    found = jnp.ones(exponents.shape, F32)
+    for power in (-2, -1, 1, 2):
+        found = jnp.where(exponents == power, 2.0 ** power, found)
+    return found
+
+
+def scale_own(stored_ref, exponents_ref, own_ref, me):
+    cols, block_count = stored_ref.shape[0], exponents_ref.shape[0]
+    block = stored_ref.shape[1] // block_count
+    span = -(-(cols + 127) // 128) * 128
+    first = jnp.minimum(me * cols // 128, (exponents_ref.shape[1] - span) // 128) * 128
+    near = exponents_ref[:, pl.ds(pl.multiple_of(first, 128), span)]
+    ahead = lax.broadcasted_iota(jnp.int32, (cols, span), 1) - lax.broadcasted_iota(
+        jnp.int32, (cols, span), 0
+    )
+    pick = jnp.where(ahead == me * cols - first, 1.0, 0.0).astype(BF16)
+    turned = dot_nt(pick, powers_of_two(near).astype(BF16))
+    for b in range(block_count):
+        here = slice(b * block, (b + 1) * block)
+        own_ref[:, here] = (stored_ref[:, here].astype(F32) * turned[:, b:b + 1]).astype(BF16)
+
+
+def place_tokens(owner_ref, candidates_ref, place_ref, picks_ref):
+    peers, tokens = picks_ref.shape[0], owner_ref.shape[1]
+    pick_count = candidates_ref.shape[0]
+    whole, _ = split_of(tokens, peers)
+    owner = owner_ref[...]
+    hot = jnp.where(lax.broadcasted_iota(jnp.int32, (peers, tokens), 0) == owner, 1.0, 0.0)
+    earlier = lax.broadcasted_iota(jnp.int32, (tokens, tokens), 0) < lax.broadcasted_iota(
+        jnp.int32, (tokens, tokens), 1
+    )
+    counts = jnp.dot(
+        hot.astype(BF16), jnp.where(earlier, 1.0, 0.0).astype(BF16), preferred_element_type=F32
+    )
+    rank = jnp.sum(counts * hot, axis=0, keepdims=True)
+    name = owner.astype(F32)
+    place_ref[...] = jnp.where(rank < whole, name * whole + rank, rank * peers + name)
+    named = candidates_ref[...].astype(F32)
+    unused = jnp.zeros((picks_ref.shape[1] - pick_count, tokens), F32)
+    named = jnp.concatenate([named, unused], axis=0).astype(BF16)
+    lanes = picks_ref.shape[2]
+    slot = lax.broadcasted_iota(jnp.int32, (lanes, tokens), 0).astype(F32)
+
+    def fill(p, _):
+        wanted = jnp.where(owner == p, rank, -1.0)
+        pick = jnp.where(slot == wanted, 1.0, 0.0).astype(BF16)
+        picks_ref[p] = dot_nt(named, pick).astype(BF16)
+        return 0
+
+    lax.fori_loop(0, peers, fill, 0)
+
+
 def front_kernel(
-    images_ref, gain_ref, q_own, p_own, mixed_ref, p_out,
+    images_far, q_stored_far, p_stored_far, q_exponents_far, p_exponents_far, owner_far,
+    candidates_far, gain_far, mixed_ref, p_out, place_ref, picks_ref,
+    images_ref, q_stored, p_stored, q_exponents, p_exponents, owner_ref, candidates_ref, gain_ref,
+    loads, q_own, p_own,
     q_all, normed, qkv, mixed, rz, ry, rx, rc, sz, sy, sx, sc, held,
 ):
     peers = q_all.shape[0]
@@ -59,6 +115,19 @@
     x = lax.axis_index("rep")
     z, y, c = me // 4, (me // 2) % 2, me % 2
     own, out = (q_own, p_own), (q_all, p_out)
+    ends = (
+        (images_far, images_ref),
+        (q_stored_far, q_stored),
+        (p_stored_far, p_stored),
+        (q_exponents_far, q_exponents),
+        (p_exponents_far, p_exponents),
+        (owner_far, owner_ref),
+        (candidates_far, candidates_ref),
+        (gain_far, gain_ref.at[0]),
+    )
+    fetched = [pltpu.make_async_copy(*end, loads.at[number]) for number, end in enumerate(ends)]
+    for number in (3, 4, 1, 2, 0, 5, 6, 7):
+        fetched[number].start()
 
     def at(zz, yy, cc):
         return (zz * 2 + yy) * 2 + cc
@@ -81,6 +150,10 @@
     def _():
         greet(to_down)
 
+    for number in (1, 2, 3, 4):
+        fetched[number].wait()
+    scale_own(q_stored, q_exponents, q_own, me)
+    scale_own(p_stored, p_exponents, p_own, me)
     greeted = 3 + jnp.where(z + 1 < nz, 1, 0) + jnp.where(z > 0, 1, 0)
     pl.semaphore_wait(barrier, greeted)
 
@@ -285,11 +358,14 @@
         return 0
 
     run(LEAD_EVENTS)
+    for number in (0, 5, 6, 7):
+        fetched[number].wait()
     normed[...] = jnp.zeros_like(normed)
     for g in range(group):
         normed[g * lanes:g * lanes + patches] = layer_norm(
             images_ref[g * patches:(g + 1) * patches], gain_ref[...]
         )
+    place_tokens(owner_ref, candidates_ref, place_ref, picks_ref)
     lax.fori_loop(0, len(QKV_EVENTS), qkv_step, 0)
     lax.fori_loop(0, group * rounds, head_step, 0)
     run(LAST_EVENTS)
@@ -327,45 +403,46 @@
 
 
 LEAD_EVENTS = ("own0", "x001", "c011",)
+LEAD_EVENTS = ("own0", "x001", "c011", "c010", "x000", "x011", "p00", "c021",)
 QKV_EVENTS = (
-    ("x000", "c010", "x011", "p00", "c021", "c020",),
     (),
-    ("c031",),
-    ("own1", "x010",),
-    ("p01", "x021",),
+    ("c020", "p01",),
+    ("x010",),
     (),
-    ("c030", "x031", "c111",),
-    ("x020",),
-    ("p02", "c121", "x101",),
-    ("c110", "p03",),
-    ("x030",),
+    ("x021", "c031", "c030",),
     (),
+    ("own1",),
+    ("x031",),
+    ("x020", "p02", "c111", "x030", "p03",),
+    ("c110",),
     (),
-    ("c131",),
-    ("c120",),
+    ("x101",),
+    (),
+    ("c121",),
+    (),
     (),
 )
 HEAD_EVENTS = (
-    (),
-    ("c130",),
-    ("p10", "x121", "x131", "x111",),
-    (),
-    (),
-    ("p13", "x120", "p12",),
-    ("p11", "x100", "x110", "x130",),
-    (),
+    ("x111", "c120",),
+    ("c131",),
+    ("x110",),
+    ("x121", "c130",),
+    ("p11", "p10", "x131", "x100",),
+    ("x120",),
+    ("x130", "p12",),
+    ("p13",),
 )
 LAST_EVENTS = ()
 
 
-def fits(images, q_own, p_own, peers, reps):
+def fits(images, q_cols, p_cols, q_blocks, peers, reps):
     tokens, width = images.shape
-    rows_whole = all(own.shape[0] % 88 == 0 for own in (q_own, p_own))
+    rows_whole = q_cols % 88 == 0 and p_cols % 88 == 0 and width == q_blocks * 128
     layout = peers == len(QKV_EVENTS) and reps == 2
-    return layout and rows_whole and width == peers * p_own.shape[0] and tokens % PATCHES == 0
-
-
-def front_call(images, gain, q_own, p_own, peers):
+    return layout and rows_whole and width == peers * p_cols and tokens % PATCHES == 0
+
+
+def front_call(images, gain, q_stored, p_stored, q_exponents, p_exponents, owner_row, candidates, peers):
     tokens, width = images.shape
     group = tokens // PATCHES
     head_dim = width // HEADS
@@ -375,14 +452,27 @@
     dma = pltpu.SemaphoreType.DMA
     return pl.pallas_call(
         front_kernel,
-        in_specs=[full] * 4,
-        out_specs=(full, pl.BlockSpec(memory_space=pl.ANY)),
+        in_specs=[pl.BlockSpec(memory_space=pltpu.HBM)] * 8,
+        out_specs=(full, pl.BlockSpec(memory_space=pl.ANY), full, full),
         out_shape=(
             jax.ShapeDtypeStruct((tokens, width), BF16),
-            jax.ShapeDtypeStruct((peers,) + p_own.shape, BF16),
+            jax.ShapeDtypeStruct((peers,) + p_stored.shape, BF16),
+            jax.ShapeDtypeStruct((1, tokens), F32),
+            jax.ShapeDtypeStruct((peers, 8, 128), BF16),
         ),
         scratch_shapes=[
-            pltpu.VMEM((peers,) + q_own.shape, BF16),
+            VMEM(images.shape, BF16),
+            VMEM(q_stored.shape, BF16),
+            VMEM(p_stored.shape, BF16),
+            VMEM(q_exponents.shape, jnp.int32),
+            VMEM(p_exponents.shape, jnp.int32),
+            VMEM(owner_row.shape, jnp.int32),
+            VMEM(candidates.shape, jnp.int32),
+            VMEM((1, width), F32),
+            dma((8,)),
+            VMEM(q_stored.shape, BF16),
+            VMEM(p_stored.shape, BF16),
+            pltpu.VMEM((peers,) + q_stored.shape, BF16),
             pltpu.VMEM((group * lanes, width), BF16),
             pltpu.VMEM((group, 3 * HEADS, head_dim, PATCHES), BF16),
             pltpu.VMEM((width, PATCHES), F32),
@@ -400,7 +490,7 @@
             collective_id=0, has_side_effects=True, vmem_limit_bytes=FRONT_LIMIT
         ),
         name="front",
-    )(images, gain, q_own, p_own)
+    )(images, q_stored, p_stored, q_exponents, p_exponents, owner_row, candidates, gain)
 
 
 def qkv_kernel(images_ref, gain_ref, w_ref, out_ref, normed):
@@ -630,7 +720,7 @@
 
     def embed(start, size):
         here = pl.ds(start, size)
-        pick = lax.broadcasted_iota(jnp.int32, (size, tokens), 0) == slot_ref[...] - start
+        pick = lax.broadcasted_iota(jnp.int32, (size, tokens), 0) == slot_ref[...].astype(jnp.int32) - start
         onehot[here, :] = jnp.where(pick, 1.0, 0.0).astype(BF16)
         mine = onehot[here, :]
         left = jnp.dot(mine, mixed_ref[...], preferred_element_type=F32).astype(BF16)
@@ -747,11 +837,12 @@
     rest_shape = (peers, 8, -(-extra * (width // 128) // 8) * 128)
     tail_shape = (peers, -(-extra * pick_count // 8) * 8, CAPT)
     anywhere = pl.BlockSpec(memory_space=pl.ANY)
+    far = pl.BlockSpec(memory_space=pltpu.HBM)
     full = pl.BlockSpec(memory_space=VMEM)
     dma = pltpu.SemaphoreType.DMA
     return pl.pallas_call(
         back_kernel,
-        in_specs=[anywhere] * 3 + [full] * 2 + [anywhere],
+        in_specs=[anywhere] * 2 + [far] + [full] * 2 + [far],
         out_specs=(anywhere, full),
         out_shape=(
             jax.ShapeDtypeStruct((tokens, width), BF16),
@@ -838,39 +929,32 @@
     me = lax.axis_index("idx")
     capacity = capacity_of(token_count, peer_count)
 
+    pick_count = candidates.shape[1]
+    gain = norm_gain[None, :]
+    qkv_cols, proj_cols = qkv_values.shape[1], proj_values.shape[1]
+    if fits(images, qkv_cols, proj_cols, qkv_exponents.shape[0], peer_count, lax.axis_size("rep")):
+        mixed, w_proj, place, picks = front_call(
+            images, norm_gain, qkv_values.T, proj_values.T, qkv_exponents, proj_exponents,
+            owners.T, candidates.T, peer_count,
+        )
+        return back_call(
+            mixed, w_proj.reshape(width, width), images, place, picks, captions, pick_count
+        )
+
     def own_exponents(exponents, cols):
         return lax.dynamic_slice_in_dim(exponents, me * cols, cols, axis=1)
 
-    qkv_cols, proj_cols = qkv_values.shape[1], proj_values.shape[1]
     qkv_own = dequant_rows(qkv_values, own_exponents(qkv_exponents, qkv_cols))
     proj_own = dequant_rows(proj_values, own_exponents(proj_exponents, proj_cols))
-    joined = fits(images, qkv_own, proj_own, peer_count, lax.axis_size("rep"))
-
     owner_ids = owners[:, 0]
     onehot = (owner_ids[:, None] == jnp.arange(peer_count, dtype=jnp.int32)[None, :]).astype(
         jnp.int32
     )
     slot_rank = jnp.sum((jnp.cumsum(onehot, axis=0) - onehot) * onehot, axis=1)
-    stride = stride_of(capacity) if joined else capacity
-    slot_index = owner_ids * stride + slot_rank
-    slots = peer_count * stride
-    pick_count = candidates.shape[1]
+    slot_index = owner_ids * capacity + slot_rank
+    slots = peer_count * capacity
     dispatch = (jnp.arange(slots, dtype=jnp.int32)[:, None] == slot_index[None, :]).astype(BF16)
     send_picks = jnp.dot(dispatch, candidates.astype(BF16), preferred_element_type=F32).astype(BF16)
-    gain = norm_gain[None, :]
-    if joined:
-        turned = send_picks.reshape(peer_count, stride, pick_count).transpose(0, 2, 1)
-        turned = jnp.pad(turned, ((0, 0), (0, 8 - pick_count), (0, 128 - stride)))
-        whole, _ = split_of(token_count, peer_count)
-        place = jnp.where(
-            slot_rank < whole,
-            owner_ids * whole + slot_rank,
-            peer_count * slot_rank + owner_ids,
-        )
-        mixed, w_proj = front_call(images, gain, qkv_own, proj_own, peer_count)
-        return back_call(
-            mixed, w_proj.reshape(width, width), images, place[None, :], turned, captions, pick_count
-        )
     w_qkv, w_proj = (lax.all_gather(own, "idx", axis=0, tiled=True) for own in (qkv_own, proj_own))
     qkv = qkv_call(images, gain, w_qkv)
     embedding, send_rows = attend_call(qkv, w_proj, images, slot_index[None, :], (slots,))

time: 145 us -> 141 us (0.972)
  other arithmetic: 5.56 us -> 0 us
  Pallas kernels: 132 us -> 137 us
  local copies, waits for them, and re-layouts: 5.02 us -> 3.44 us
    pallas_call x2, Pallas kernels: 132 us -> 137 us  [the longest x1 79.2 us: front_call(): pl.pallas_call(front_kernel, in_specs=[pl.BlockSpec(memory_space=pltpu.HB...]
    transpose x2 -> x0, other arithmetic: 1.64 us -> none  [dequant_rows(): scaled = turned * jnp.exp2(exponents.astype(F32)).T[:, :, None]]
    another operation x4 -> x0, other arithmetic: 1.54 us -> none
    unnamed x10 -> x4, local copies, waits for them, and re-layouts: 2.87 us -> 3.44 us
where the time goes in v3:
time: 141 us
  Pallas kernels  137 us (97%)
  local copies, waits for them, and re-layouts  3.44 us (2%)
    pallas_call x1, Pallas kernels, front_call(): pl.pallas_call(front_kernel, in_specs=[pl.BlockSpec(memory_space=pltpu.HB...  79.2 us
    pallas_call x1, Pallas kernels, back_call(): pl.pallas_call(back_kernel, in_specs=[anywhere] * 2 + [far] + [full] * 2...  57.8 us
    unnamed x4, local copies, waits for them, and re-layouts  3.44 us

profile of v3, /device:TPU:0, one launch (start us, length us, event | category | flops | bytes accessed | tf_op | source)
XLA Modules:
  0.0 141.1 jit_solution(4353721949570690690)
XLA Ops:
  0.6 79.2 %front.1 = (bf16[514,1408]{1,0:T(8,128)(2,1)}, bf16[16,88,1408]{2,1,0:T(8,128)(2,1)}, f32[1,514]{1,0:T(1,128)}, bf16[16,8,128]{2,1,0:T(8,128)(2,1)}) custom-call(bf16[514,1408]{1,0:T(8,128)(2,1)} %images_far.3, bf16[264,1408]{1,0:T(8,128)(2,1)} %bitcast.6, bf16[88,1408]{1,0:T(8,128)(2,1)} %bitcast.7, s32[11,4224]{1,0:T(8,128)} %q_exponents_far.1, ...), custom_call_target="tpu_custom_call" | custom-call | tf_op jit(solution)/shard_map/front/pallas_call | solution.py:453
  79.8 57.8 %back.1 = (bf16[514,1408]{1,0:T(8,128)(2,1)}, bf16[514,4,128]{2,1,0:T(4,128)(2,1)}) custom-call(bf16[514,1408]{1,0:T(8,128)(2,1)} %get-tuple-element.6.mixed_far, bf16[1408,1408]{1,0:T(8,128)(2,1)} %bitcast.5, bf16[514,1408]{1,0:T(8,128)(2,1)} %images_far.3, f32[1,514]{1,0:T(1,128)} %get-tuple-element.8.slot_ref, ...), custom_call_target="tpu_custom_call" | custom-call | tf_op jit(solution)/shard_map/back/pallas_call | solution.py:843
  137.6 0.0 copy-start
  137.6 2.6 %copy.13 = bf16[514,1408]{1,0:T(8,128)(2,1)} copy(bf16[514,1408]{1,0:T(8,128)(2,1)} %get-tuple-element.12) | data formatting | bytes 2894848
  140.3 0.0 copy-done
  140.3 0.8 copy.14
Async XLA Ops:
  137.6 2.7 %copy-start = (bf16[514,4,128]{2,1,0:T(4,128)(2,1)S(1)}, bf16[514,4,128]{2,1,0:T(4,128)(2,1)}, u32[]{:S(2)}) copy-start(bf16[514,4,128]{2,1,0:T(4,128)(2,1)} %get-tuple-element.13) | copy-start | bytes 1579012
